TPU v7x, 32 devices: a whole 2x2x4 slice. The times are simulated.
32 devices in a mesh: grp: 2 (over x), pool: 16 (over z, y, core).
Axes of the slice: x: 2, y: 2, z: 4, core: 2. Of those that a mesh axis runs over, the one named last changes fastest.
Arguments:
- queries: bfloat16 [32, 128, 1024], P(('grp', 'pool')), parts along dimension 0, may hold values from -400 to 400
- new_kv: bfloat16 [32, 128, 256], P(('grp', 'pool')), parts along dimension 0, may hold values from -16 to 16
- pool_kv: bfloat16 [64, 8, 128, 256], P(('grp', 'pool')), parts along dimension 0, may hold values from -16 to 16
- hit_slots: int32 [4, 16], P('grp'), parts along dimension 0, may hold values from 0 to 31, as said below
- prefix_blocks: int32 [4], P('grp'), parts along dimension 0, may hold values from 1 to 16, 20 in all
- new_owners: int32 [4, 2], P('grp'), parts along dimension 0, may hold values from 0 to 15, as said below
Outputs:
- attended: bfloat16 [32, 128, 1024], P(('grp', 'pool')), parts along dimension 0
- new_store: bfloat16 [32, 8, 128, 256], P(('grp', 'pool')), parts along dimension 0
There are 2 independent parts, one for each index of `grp`. A program takes and returns all parts, laid end to end along the dimension named above; each array names one. Nothing has to cross between parts.
Inputs may be any that keep to these rules, and one draw needn't show every extreme that they name: `hit_slots`: slot s lies on owner s // 2. Block j of request r lies on owner (f + j) mod 16, where f depends on r and is a multiple of 4; one owner keeps different requests in different slots. Entries with j >= prefix_blocks[r] are unused. `prefix_blocks`: they sum to 20. `new_owners`: all 4 entries are distinct.
All inputs are finite; a program needn't handle non-finite values.
Results may differ from a plain program's by a relative error of at most 0.009.
Values may be sent and summed in bfloat16 or wider, within the bound.
No kernel may reach another device: no remote copies, remote signals or barrier semaphores. Data moves between devices by JAX's collectives and lax.ppermute only.
A program may use at most 64 MiB of HBM per device.

v0:
```python
import math

import jax
import jax.numpy as jnp
from jax import lax
from jax.sharding import PartitionSpec as P

group_slots = 4
minus_big = -1e30


def fold_keys(state_now, query_rows, key_rows, values, usable, score_scale):
    maximum, totals, accumulated = state_now
    scores = (
        jnp.einsum("tgd,kd->tgk", query_rows, key_rows, preferred_element_type=jnp.float32)
        * score_scale
    )
    scores = jnp.where(usable, scores, minus_big)
    maximum_new = jnp.maximum(maximum, jnp.max(scores, axis=2))
    weights = jnp.where(usable, jnp.exp(scores - maximum_new[:, :, None]), 0.0)
    factor = jnp.exp(maximum - maximum_new)
    totals = totals * factor + jnp.sum(weights, axis=2)
    accumulated = accumulated * factor[:, :, None] + jnp.einsum(
        "tgk,kd->tgd", weights.astype(jnp.bfloat16), values, preferred_element_type=jnp.float32
    )
    return (maximum_new, totals, accumulated)


def attend_blocks(state_now, query_rows, stored, first_slot, live_count, score_scale):
    slot_total = stored.shape[0]
    block_len = stored.shape[1]
    row_width = stored.shape[2]
    head_dim = row_width // 2
    loop_steps = (live_count + group_slots - 1) // group_slots
    offsets = jnp.arange(group_slots * block_len, dtype=jnp.int32) // block_len

    def advance(turn_index, state_in):
        start_slot = (first_slot + turn_index * group_slots) % slot_total
        block_rows = lax.dynamic_slice_in_dim(stored, start_slot, group_slots, 0).reshape(
            group_slots * block_len, row_width
        )
        usable = (turn_index * group_slots + offsets < live_count)[None, None, :]
        return fold_keys(
            state_in,
            query_rows,
            block_rows[:, :head_dim],
            block_rows[:, head_dim:],
            usable,
            score_scale,
        )

    return lax.fori_loop(0, loop_steps, advance, state_now)


def on_device(queries, new_kv, pool_kv, hit_slots, prefix_blocks, new_owners):
    my_index = lax.axis_index("pool")
    slot_count = pool_kv.shape[0]
    kv_heads = pool_kv.shape[1]
    block_len = pool_kv.shape[2]
    row_width = pool_kv.shape[3]
    head_dim = row_width // 2
    requests = hit_slots.shape[0]
    longest = hit_slots.shape[1]
    groups = queries.shape[2] // head_dim
    score_scale = 1.0 / math.sqrt(head_dim)
    request = my_index // kv_heads
    positions = jnp.arange(longest, dtype=jnp.int32)
    is_live = positions[None, :] < prefix_blocks[:, None]
    on_me = (hit_slots // slot_count == my_index) & is_live
    holds_block = jnp.any(on_me, axis=1)
    local_slot = jnp.sum(jnp.where(on_me, hit_slots % slot_count, 0), axis=1)
    picked = jnp.take(pool_kv, local_slot, axis=0)
    outgoing = jnp.where(holds_block[:, None, None, None], picked, jnp.zeros_like(picked))
    outgoing = outgoing.reshape(requests * kv_heads, block_len, row_width)
    fetched = lax.all_to_all(outgoing, "pool", split_axis=0, concat_axis=0, tiled=True)
    query_rows = queries[0].reshape(block_len, groups, head_dim)
    own_new = new_kv[0]
    causal = (jnp.arange(block_len)[None, :] <= jnp.arange(block_len)[:, None])[:, None, :]
    empty_state = (
        jnp.full((block_len, groups), minus_big, jnp.float32),
        jnp.zeros((block_len, groups), jnp.float32),
        jnp.zeros((block_len, groups, head_dim), jnp.float32),
    )
    state_now = fold_keys(
        empty_state, query_rows, own_new[:, :head_dim], own_new[:, head_dim:], causal, score_scale
    )
    own_length = prefix_blocks[request]
    own_first = hit_slots[request, 0] // slot_count
    state_now = attend_blocks(state_now, query_rows, fetched, own_first, own_length, score_scale)
    attended = (
        (state_now[2] / state_now[1][:, :, None])
        .reshape(block_len, groups * head_dim)
        .astype(jnp.bfloat16)[None]
    )
    arrived = lax.all_gather(new_kv, "pool", axis=0, tiled=True)
    owned_by_me = jnp.any(new_owners == my_index, axis=1)
    source_request = jnp.sum(jnp.where(owned_by_me, jnp.arange(requests, dtype=jnp.int32), 0))
    owned = jnp.any(owned_by_me)
    new_block = lax.dynamic_slice_in_dim(arrived, source_request * kv_heads, kv_heads, 0)
    new_store = jnp.where(owned, new_block, jnp.zeros_like(new_block))[None]
    return (attended, new_store)


def solution(mesh):
    placed = (
        P(("grp", "pool"), None, None),
        P(("grp", "pool"), None, None),
        P(("grp", "pool"), None, None, None),
        P("grp", None),
        P("grp"),
        P("grp", None),
    )
    return jax.shard_map(
        on_device,
        mesh=mesh,
        in_specs=placed,
        out_specs=(P(("grp", "pool"), None, None), P(("grp", "pool"), None, None, None)),
        check_vma=False,
    )
```

profile of v0, /device:TPU:0, one launch (start us, length us, event | category | flops | bytes accessed | tf_op | source)
XLA Modules:
  0.0 74.9 jit_solution(3903400085508740048)
XLA Ops:
  7.2 1.0 %fusion.36 = (pred[2]{0:T(512)(128)(4,1)S(1)}, pred[2,16]{1,0:T(4,128)(4,1)S(1)}) fusion(s32[2]{0:T(128)} %param.12, s32[]{:T(128)S(6)} %axis_index.12, s32[2,16]{1,0:T(2,128)} %param.11), kind=kLoop, calls=%fused_computation.73 | loop fusion | flops 606 | bytes 174 | tf_op jit(solution)/shard_map/reduce_or | solution.py:70
  8.2 0.8 %fusion.30 = s32[2]{0:T(128)S(1)} fusion(pred[2,16]{1,0:T(4,128)(4,1)S(1)} %get-tuple-element.196, s32[2,16]{1,0:T(2,128)} %param.11), kind=kLoop, calls=%fused_computation.62 | loop fusion | flops 414 | bytes 168 | tf_op jit(solution)/shard_map/reduce_sum | solution.py:71
  9.3 0.6 gather_fusion
  10.0 1.3 %fusion.22 = bf16[16,128,256]{2,1,0:T(8,128)(2,1)} fusion(bf16[2,8,128,256]{3,2,1,0:T(8,128)(2,1)S(1)} %gather_fusion, pred[16]{0:T(512)(128)(4,1)S(1)} %broadcast_in_dim.118, pred[16]{0:T(512)(128)(4,1)S(1)} %broadcast_in_dim.115), kind=kLoop, calls=%fused_computation.37 | loop fusion | flops 1048576 | bytes 2097184 | tf_op jit(solution)/shard_map/jit(_where)/select_n | solution.py:73
  11.3 7.5 %all-to-all-start = ((bf16[16,128,256]{2,1,0:T(8,128)(2,1)}), bf16[16,128,256]{2,1,0:T(8,128)(2,1)S(1)}, u32[]{:S(2)}, u32[]{:S(2)}) async-start(bf16[16,128,256]{2,1,0:T(8,128)(2,1)} %fusion.22), calls=%async_computation | async-start | bytes 2097152 | tf_op jit(solution)/shard_map/all_to_all | solution.py:75
  18.9 0.7 all-gather.2.cloned.1.call-update
  19.6 0.5 constant_dynamic-slice_fusion.1
  22.7 0.6 dynamic_slice.15
  24.4 0.7 fusion.34
  25.0 0.7 select_reduce_fusion
  27.1 15.8 %all-to-all-done = bf16[16,128,256]{2,1,0:T(8,128)(2,1)S(1)} async-done(((bf16[16,128,256]{2,1,0:T(8,128)(2,1)}), bf16[16,128,256]{2,1,0:T(8,128)(2,1)S(1)}, u32[]{:S(2)}, u32[]{:S(2)}) %all-to-all-start) | async-done | bytes 1048608 | tf_op jit(solution)/shard_map/all_to_all | solution.py:75
  42.8 8.5 %while.17 = (s32[]{:T(128)}, f32[128,8]{0,1:T(8,128)S(1)}, f32[128,8]{0,1:T(8,128)S(1)}, f32[128,8,128]{2,0,1:T(8,128)S(1)}, s32[]{:T(128)}, /*index=5*/s32[]{:T...) while((s32[]{:T(128)}, f32[128,8]{0,1:T(8,128)S(1)}, ...), condition=%wide.region_7.8_spmd.clone, body=%wide.region_4.7_spmd.clone.sunk | while | flops 275520512 | bytes 8457016 | solution.py:52
  42.8 0.7 fusion.46
  44.0 0.6 fusion.47
  44.6 1.0 %convolution_add_fusion.3 = f32[128,8,128]{2,0,1:T(8,128)S(1)} fusion(f32[512,128,8]{1,0,2:T(8,128)S(1)} %get-tuple-element.264, f32[128,8]{0,1:T(8,128)S(1)} %max.8, pred[512]{0:T(512)(128)(4,1)S(1)} %fusion.46, f32[128,8,128]{2,0,1:T(8,128)S(1)} %get-tuple-element.284, f32[128,8]{0,1:T(8,128)S(1)} %get-tuple-element.266, ...), kind=kOutput, calls=%fused_computation.9.clone.1 | convolution fusion | flops 137101312 | bytes 3286016 | tf_op jit(solution)/shard_map/while/body/tgk,kd->tgd/dot_general | solution.py:23
  45.7 0.7 fusion.46
  46.9 0.6 fusion.47
  47.5 1.0 %convolution_add_fusion.3 = f32[128,8,128]{2,0,1:T(8,128)S(1)} fusion(f32[512,128,8]{1,0,2:T(8,128)S(1)} %get-tuple-element.264, f32[128,8]{0,1:T(8,128)S(1)} %max.8, pred[512]{0:T(512)(128)(4,1)S(1)} %fusion.46, f32[128,8,128]{2,0,1:T(8,128)S(1)} %get-tuple-element.284, f32[128,8]{0,1:T(8,128)S(1)} %get-tuple-element.266, ...), kind=kOutput, calls=%fused_computation.9.clone.1 | convolution fusion | flops 137101312 | bytes 3286016 | tf_op jit(solution)/shard_map/while/body/tgk,kd->tgd/dot_general | solution.py:23
  48.6 0.7 fusion.46
  49.7 0.6 fusion.47
  50.3 1.0 %convolution_add_fusion.3 = f32[128,8,128]{2,0,1:T(8,128)S(1)} fusion(f32[512,128,8]{1,0,2:T(8,128)S(1)} %get-tuple-element.264, f32[128,8]{0,1:T(8,128)S(1)} %max.8, pred[512]{0:T(512)(128)(4,1)S(1)} %fusion.46, f32[128,8,128]{2,0,1:T(8,128)S(1)} %get-tuple-element.284, f32[128,8]{0,1:T(8,128)S(1)} %get-tuple-element.266, ...), kind=kOutput, calls=%fused_computation.9.clone.1 | convolution fusion | flops 137101312 | bytes 3286016 | tf_op jit(solution)/shard_map/while/body/tgk,kd->tgd/dot_general | solution.py:23
  51.8 0.8 %convert_element_type.24 = bf16[1,128,1024]{2,1,0:T(8,128)(2,1)} reshape(bf16[128,8,128]{2,1,0:T(8,128)(2,1)S(1)} %copy.22) | data formatting | bytes 524288 | tf_op jit(solution)/shard_map/convert_element_type | solution.py:93
  52.6 13.0 %all-gather.2.cloned.1.call-done = bf16[16,128,256]{2,1,0:T(8,128)(2,1)} async-done(((bf16[1,128,256]{2,1,0:T(8,128)(2,1)}), bf16[16,128,256]{2,1,0:T(8,128)(2,1)}) %all-gather.2.cloned.1.call-update) | async-done | bytes 1048592 | tf_op jit(solution)/shard_map/all_gather | solution.py:95
  65.6 2.5 %select_bitcast_fusion = bf16[1,8,128,256]{3,2,1,0:T(8,128)(2,1)} fusion(bf16[16,128,256]{2,1,0:T(8,128)(2,1)} %all-gather.2.cloned.1.call-done, s32[]{:T(128)S(6)} %select_n.133, pred[]{:T(512)} %get-tuple-element.173), kind=kLoop, calls=%fused_computation.38 | loop fusion | flops 262144 | bytes 1048581 | tf_op jit(solution)/shard_map/broadcast_in_dim | solution.py:100
  (45 shorter events, 3.4 us)
Async XLA Ops:
  7.2 2.1 %copy-start = (bf16[2,8,128,256]{3,2,1,0:T(8,128)(2,1)S(1)}, bf16[2,8,128,256]{3,2,1,0:T(8,128)(2,1)}, u32[]{:S(2)}) copy-start(bf16[2,8,128,256]{3,2,1,0:T(8,128)(2,1)} %param.10) | copy-start | bytes 3145732
  9.9 9.6 %copy-start.3 = (s32[2,16]{1,0:T(2,128)S(1)}, s32[2,16]{1,0:T(2,128)}, u32[]{:S(2)}) copy-start(s32[2,16]{1,0:T(2,128)} %param.11) | copy-start | bytes 388
  9.9 12.8 %copy-start.5 = (s32[2]{0:T(128)S(1)}, s32[2]{0:T(128)}, u32[]{:S(2)}) copy-start(s32[2]{0:T(128)} %param.12) | copy-start | bytes 28
  10.0 14.0 %copy-start.2 = (bf16[1,128,1024]{2,1,0:T(8,128)(2,1)S(1)}, bf16[1,128,1024]{2,1,0:T(8,128)(2,1)}, u32[]{:S(2)}) copy-start(bf16[1,128,1024]{2,1,0:T(8,128)(2,1)} %param.8) | copy-start | bytes 786436
  11.3 13.1 %copy-start.4 = (s32[2,2]{1,0:T(2,128)S(1)}, s32[2,2]{1,0:T(2,128)}, u32[]{:S(2)}) copy-start(s32[2,2]{1,0:T(2,128)} %param.13) | copy-start | bytes 52
  11.3 15.1 %copy-start.1 = (bf16[1,128,256]{2,1,0:T(8,128)(2,1)S(1)}, bf16[1,128,256]{2,1,0:T(8,128)(2,1)}, u32[]{:S(2)}) copy-start(bf16[1,128,256]{2,1,0:T(8,128)(2,1)} %param.9) | copy-start | bytes 196612
  11.3 31.6 %all-to-all-start = ((bf16[16,128,256]{2,1,0:T(8,128)(2,1)}), bf16[16,128,256]{2,1,0:T(8,128)(2,1)S(1)}, u32[]{:S(2)}, u32[]{:S(2)}) async-start(bf16[16,128,256]{2,1,0:T(8,128)(2,1)} %fusion.22), calls=%async_computation | async-start | bytes 2097152 | tf_op jit(solution)/shard_map/all_to_all | solution.py:75
  18.8 46.8 %all-gather.2.cloned.1.call-start = ((), (), s32[]{:S(2)}) async-start(), calls=%async_computation.1 | async-start | bytes 1114112 | tf_op jit(solution)/shard_map/all_gather | solution.py:95
Sparse Core Ops, SparseCore 0:
  21.8 43.7 all-gather.1
where the time goes:
time: 75.3 us; the launch traced here: 74.9 us
  waiting for transfers between devices  29.4 us (39%)
  between operations  18.1 us (24%)
  other arithmetic  11.1 us (15%)
  starting transfers between devices  7.59 us (10%)
  matrix products  4.96 us (7%)
  local copies, waits for them, and re-layouts  3.49 us (5%)
    all_to_all x1, waiting for transfers between devices, on_device(): lax.all_to_all(outgoing, 'pool', split_axis=0, concat_axis=0, tiled=True)  15.8 us
    all_gather x1, waiting for transfers between devices, on_device(): arrived = lax.all_gather(new_kv, 'pool', axis=0, tiled=True)  13 us
    all_to_all x1, starting transfers between devices, on_device(): lax.all_to_all(outgoing, 'pool', split_axis=0, concat_axis=0, tiled=True)  7.55 us
    dot_general x4, matrix products, fold_keys(): jnp.einsum('tgk,kd->tgd', weights.astype(jnp.bfloat16), values, preferred...  3.33 us
    broadcast_in_dim x1, other arithmetic, on_device(): new_store = jnp.where(owned, new_block, jnp.zeros_like(new_block))[None]  2.49 us
    lt x3, other arithmetic, advance(): usable = (turn_index * group_slots + offsets < live_count)[None, None, :]  1.96 us
    reduce_sum x4, other arithmetic, fold_keys(): totals = totals * factor + jnp.sum(weights, axis=2)  1.92 us
    dot_general x4, matrix products, fold_keys(): jnp.einsum('tgd,kd->tgk', query_rows, key_rows, preferred_element_type=jn...  1.63 us
  transfers between devices with their start and end apart: 2, of which 2 were waited for; matrix products, arithmetic and copies ran while one was open for 17% of the time, Pallas kernels for 0%

commit v1 on v0

v1 whole, which is shorter than its diff:
```python
import functools
import math

import jax
import jax.numpy as jnp
from jax import lax
from jax.experimental import pallas as pl
from jax.experimental.pallas import tpu as pltpu
from jax.sharding import PartitionSpec as P

MINUS_BIG = -1e30
ANY = pl.BlockSpec(memory_space=pl.ANY)
SMEM = pl.BlockSpec(memory_space=pltpu.SMEM)


def owner_position(hits_ref, request, owner, slots, pool):
    first = hits_ref[request, 0] // slots
    return lax.rem(owner - first + pool, pool)


def held_slot(hits_ref, blocks_ref, request, me, slots, pool):
    position = owner_position(hits_ref, request, me, slots, pool)
    longest = hits_ref.shape[1]
    entry = hits_ref[request, jnp.minimum(position, longest - 1)]
    return jnp.where(position < blocks_ref[request], lax.rem(entry, slots), 0)


def wanted_request(owners_ref, device):
    found = jnp.int32(0)
    any_found = jnp.bool_(False)
    for request in range(owners_ref.shape[0]):
        for copy in range(owners_ref.shape[1]):
            hit = owners_ref[request, copy] == device
            found = jnp.where(hit, request, found)
            any_found = jnp.logical_or(any_found, hit)
    return found, any_found


def pack_far_kernel(plan, sizes, hits_ref, blocks_ref, pool_ref, *rest):
    slots, heads, pool = sizes
    outs, (stage, in_sems, out_sems) = rest[: len(plan)], rest[len(plan) :]
    me = lax.axis_index("pool")
    loads = []
    row = 0
    for index, targets in enumerate(plan):
        for place, k in enumerate(targets):
            other = lax.bitwise_xor(me, k)
            request = other // heads
            slot = held_slot(hits_ref, blocks_ref, request, me, slots, pool)
            load = pltpu.make_async_copy(
                pool_ref.at[slot, lax.rem(other, heads)], stage.at[row], in_sems.at[row]
            )
            load.start()
            loads.append((load, row, index, place))
            row += 1
    stores = []
    for load, row, index, place in loads:
        load.wait()
        store = pltpu.make_async_copy(stage.at[row], outs[index].at[place], out_sems.at[row])
        store.start()
        stores.append(store)
    for store in stores:
        store.wait()


def pack_far(plan, hits, blocks, pool_kv, pool):
    slots, heads, length, width = pool_kv.shape
    rows = sum(len(targets) for targets in plan)
    return pl.pallas_call(
        functools.partial(pack_far_kernel, plan, (slots, heads, pool)),
        out_shape=[
            jax.ShapeDtypeStruct((len(targets), length, width), pool_kv.dtype) for targets in plan
        ],
        in_specs=[SMEM, SMEM, ANY],
        out_specs=[ANY] * len(plan),
        scratch_shapes=[
            pltpu.VMEM((rows, length, width), pool_kv.dtype),
            pltpu.SemaphoreType.DMA((rows,)),
            pltpu.SemaphoreType.DMA((rows,)),
        ],
        name="pack_far",
    )(hits, blocks, pool_kv)


def pack_near_kernel(near, sizes, hits_ref, blocks_ref, owners_ref, pool_ref, *rest):
    slots, heads, pool, requests = sizes
    news, rest = rest[:requests], rest[requests:]
    outs, (stage, fresh, in_sems, fresh_sems, out_sems) = rest[: len(near)], rest[len(near) :]
    me = lax.axis_index("pool")
    mine = me // heads
    fresh_loads = []
    for m in range(requests):
        load = pltpu.make_async_copy(news[m].at[0], fresh.at[m], fresh_sems.at[m])
        load.start()
        fresh_loads.append(load)
    slot = held_slot(hits_ref, blocks_ref, mine, me, slots, pool)
    loads = []
    for index, k in enumerate(near):
        other = lax.bitwise_xor(me, k)
        load = pltpu.make_async_copy(
            pool_ref.at[slot, lax.rem(other, heads)], stage.at[index], in_sems.at[index]
        )
        load.start()
        loads.append(load)
    for load in fresh_loads:
        load.wait()
    stores = []
    for index, k in enumerate(near):
        wanted, _ = wanted_request(owners_ref, lax.bitwise_xor(me, k))
        store = pltpu.make_async_copy(
            fresh.at[lax.bitwise_xor(wanted, mine)], outs[index].at[1], out_sems.at[2 * index]
        )
        store.start()
        stores.append(store)
    for index, k in enumerate(near):
        loads[index].wait()
        store = pltpu.make_async_copy(
            stage.at[index], outs[index].at[0], out_sems.at[2 * index + 1]
        )
        store.start()
        stores.append(store)
    for store in stores:
        store.wait()


def pack_near(near, hits, blocks, owners, pool_kv, news, pool):
    slots, heads, length, width = pool_kv.shape
    count = len(near)
    return pl.pallas_call(
        functools.partial(pack_near_kernel, near, (slots, heads, pool, len(news))),
        out_shape=[jax.ShapeDtypeStruct((2, length, width), pool_kv.dtype)] * count,
        in_specs=[SMEM, SMEM, SMEM, ANY] + [ANY] * len(news),
        out_specs=[ANY] * count,
        scratch_shapes=[
            pltpu.VMEM((count, length, width), pool_kv.dtype),
            pltpu.VMEM((len(news), length, width), pool_kv.dtype),
            pltpu.SemaphoreType.DMA((count,)),
            pltpu.SemaphoreType.DMA((len(news),)),
            pltpu.SemaphoreType.DMA((2 * count,)),
        ],
        name="pack_near",
    )(hits, blocks, owners, pool_kv, *news)


def store_new_kernel(near, sizes, owners_ref, *rest):
    heads, requests = sizes
    news, rest = rest[:requests], rest[requests:]
    pieces, rest = rest[: len(near)], rest[len(near) :]
    out_ref, stage, in_sems, out_sems = rest
    me = lax.axis_index("pool")
    mine = me // heads
    head = lax.rem(me, heads)
    wanted, owned = wanted_request(owners_ref, me)

    @pl.when(owned)
    def _():
        for m in range(requests):
            @pl.when(lax.bitwise_xor(wanted, mine) == m)
            def _(m=m):
                pltpu.make_async_copy(news[m].at[0], stage.at[0], in_sems.at[0]).start()
        for index, _k in enumerate(near):
            load = pltpu.make_async_copy(
                pieces[index].at[1], stage.at[1 + index], in_sems.at[1 + index]
            )
            load.start()
        for index in range(len(near) + 1):
            pltpu.make_async_copy(news[0].at[0], stage.at[index], in_sems.at[index]).wait()

    @pl.when(jnp.logical_not(owned))
    def _():
        stage[...] = jnp.zeros_like(stage)

    stores = []
    for index, k in enumerate((0,) + tuple(near)):
        store = pltpu.make_async_copy(
            stage.at[index], out_ref.at[0, lax.bitwise_xor(head, k)], out_sems.at[index]
        )
        store.start()
        stores.append(store)
    for store in stores:
        store.wait()


def store_new(near, owners, news, pieces, heads):
    _, length, width = news[0].shape
    count = len(near) + 1
    return pl.pallas_call(
        functools.partial(store_new_kernel, near, (heads, len(news))),
        out_shape=jax.ShapeDtypeStruct((1, heads, length, width), news[0].dtype),
        in_specs=[SMEM] + [ANY] * (len(news) + len(pieces)),
        out_specs=ANY,
        scratch_shapes=[
            pltpu.VMEM((count, length, width), news[0].dtype),
            pltpu.SemaphoreType.DMA((count,)),
            pltpu.SemaphoreType.DMA((count,)),
        ],
        name="store_new",
    )(owners, *news, *pieces)


def attend_kernel(keys, sizes, first, last, hits_ref, blocks_ref, query_ref, *rest):
    slots, heads, pool, arrays = sizes
    kv_refs, rest = rest[:arrays], rest[arrays:]
    if not first:
        (acc_in, stat_in), rest = rest[:2], rest[2:]
    if last:
        (out_ref,), rest = rest[:1], rest[1:]
    else:
        (acc_out, stat_out), rest = rest[:2], rest[2:]
    kv, kv_sems = rest
    me = lax.axis_index("pool")
    request = me // heads
    length = query_ref.shape[1]
    width = kv.shape[1]
    head_dim = width // 2
    groups = query_ref.shape[2] // head_dim
    loads = []
    for index, (_k, array, place) in enumerate(keys):
        load = pltpu.make_async_copy(
            kv_refs[array].at[place], kv.at[pl.ds(index * length, length)], kv_sems.at[index]
        )
        load.start()
        loads.append(load)
    alive = []
    for k, _array, _place in keys:
        if k is None:
            alive.append(None)
        else:
            position = owner_position(hits_ref, request, lax.bitwise_xor(me, k), slots, pool)
            alive.append(position < blocks_ref[request])
    for load in loads:
        load.wait()
    to_exponent = math.log2(math.e) / math.sqrt(head_dim)
    causal = lax.broadcasted_iota(jnp.int32, (length, length), 1) <= lax.broadcasted_iota(
        jnp.int32, (length, length), 0
    )
    for group in range(groups):
        rows = slice(group * length, (group + 1) * length)
        query = query_ref[0, :, group * head_dim : (group + 1) * head_dim]
        scores = lax.dot_general(
            query,
            kv[:, :head_dim],
            (((1,), (1,)), ((), ())),
            preferred_element_type=jnp.float32,
        )
        parts = []
        for index, live in enumerate(alive):
            part = scores[:, index * length : (index + 1) * length]
            parts.append(jnp.where(causal if live is None else live, part, MINUS_BIG))
        scores = jnp.concatenate(parts, 1)
        top = jnp.max(scores, axis=1, keepdims=True)
        if not first:
            old = stat_in[rows, :]
            old_top = old[:, :1]
            old_total = old[:, head_dim // 2 : head_dim // 2 + 1]
            top = jnp.maximum(top, old_top)
            factor = jnp.exp2((old_top - top) * to_exponent)
        weights = jnp.exp2((scores - top) * to_exponent)
        total = jnp.sum(weights, axis=1, keepdims=True)
        mixed = lax.dot_general(
            weights.astype(jnp.bfloat16),
            kv[:, head_dim:],
            (((1,), (0,)), ((), ())),
            preferred_element_type=jnp.float32,
        )
        if not first:
            total = total + old_total * factor
            mixed = mixed + acc_in[rows, :] * factor
        if last:
            out_ref[0, :, group * head_dim : (group + 1) * head_dim] = (mixed / total).astype(
                out_ref.dtype
            )
        else:
            acc_out[rows, :] = mixed
            lane = lax.broadcasted_iota(jnp.int32, (length, head_dim), 1)
            stat_out[rows, :] = jnp.where(lane < head_dim // 2, top, total)


def attend(keys, hits, blocks, queries, arrays, state, last, slots, heads, pool):
    _, length, columns = queries.shape
    width = arrays[0].shape[-1]
    head_dim = width // 2
    rows = columns // head_dim * length
    first = state is None
    whole = pl.BlockSpec(memory_space=pltpu.VMEM)
    state_shape = jax.ShapeDtypeStruct((rows, head_dim), jnp.float32)
    scores = rows * len(keys) * length
    return pl.pallas_call(
        functools.partial(attend_kernel, keys, (slots, heads, pool, len(arrays)), first, last),
        out_shape=jax.ShapeDtypeStruct(queries.shape, queries.dtype)
        if last
        else (state_shape, state_shape),
        in_specs=[SMEM, SMEM, whole] + [ANY] * len(arrays) + ([] if first else [whole] * 2),
        out_specs=whole if last else (whole, whole),
        scratch_shapes=[
            pltpu.VMEM((len(keys) * length, width), jnp.bfloat16),
            pltpu.SemaphoreType.DMA((len(keys),)),
        ],
        cost_estimate=pl.CostEstimate(
            flops=4 * scores * head_dim,
            bytes_accessed=4 * rows * width,
            transcendentals=scores,
        ),
    )(hits, blocks, queries, *arrays, *(() if first else state))


def on_device(sizes, queries, new_kv, pool_kv, hits, blocks, owners):
    pool, far_pairs, far_last, near = sizes
    slots, heads, _, _ = pool_kv.shape
    requests = hits.shape[0]

    def swap(k, array):
        return lax.ppermute(array, "pool", [(p, p ^ k) for p in range(pool)])

    news = [new_kv] + [swap(m * heads, new_kv) for m in range(1, requests)]
    plan = [(k, k ^ 1) for k in far_pairs] + [(k,) for k in far_last]
    *packed, own = pack_far([*plan, (0,)], hits, blocks, pool_kv, pool)
    far = [swap(k[0], array) for k, array in zip(plan, packed)]
    near_packed = pack_near(near, hits, blocks, owners, pool_kv, news, pool)
    pieces = [swap(k, array) for k, array in zip(near, near_packed)]
    mates = [swap(1, array) for k, array in zip(plan, far) if len(k) == 2]
    common = dict(slots=slots, heads=heads, pool=pool)
    keys = [(None, 0, 0), (0, 1, 0)] + [(k, 2 + i, 0) for i, k in enumerate(near)]
    state = attend(
        keys, hits, blocks, queries, [new_kv, own, *pieces], None, False,
        **common,
    )
    new_store = store_new(near, owners, news, pieces, heads)
    count = len(far_pairs)
    keys = [(k, i, 0) for i, k in enumerate(far_pairs)]
    keys += [(k ^ 1, count + i, 1) for i, k in enumerate(far_pairs)]
    state = attend(
        keys, hits, blocks, queries, [*far[:count], *mates], state, False,
        **common,
    )
    keys = [(k, i, 0) for i, k in enumerate(far_last)]
    attended = attend(
        keys, hits, blocks, queries, far[count:], state, True,
        **common,
    )
    return attended, new_store


def solution(mesh):
    pool = mesh.shape["pool"]
    placed = (
        P(("grp", "pool"), None, None),
        P(("grp", "pool"), None, None),
        P(("grp", "pool"), None, None, None),
        P("grp", None),
        P("grp"),
        P("grp", None),
    )

    def whole(queries, new_kv, pool_kv, hits, blocks, owners):
        heads = pool_kv.shape[1]
        far_all = list(range(heads, pool, 2))
        far_all = far_all[len(far_all) // 2 :] + far_all[: len(far_all) // 2]
        far_pairs, final = far_all[:-1], far_all[-1]
        far_last = [final, final ^ 1]
        near = tuple(range(1, heads))
        sizes = (pool, far_pairs, far_last, near)
        step = jax.shard_map(
            functools.partial(on_device, sizes),
            mesh=mesh,
            in_specs=placed,
            out_specs=(P(("grp", "pool"), None, None), P(("grp", "pool"), None, None, None)),
            check_vma=False,
        )
        return step(queries, new_kv, pool_kv, hits, blocks, owners)

    return whole
```

time: 75.3 us -> 73.1 us (0.971); the launches traced: 74.9 us -> 71.8 us
  Pallas kernels: 0 us -> 26.2 us
  between operations: 18.1 us -> 0.86 us
  other arithmetic: 11.1 us -> 0 us
  starting transfers between devices: 7.59 us -> 18.2 us
  matrix products: 4.96 us -> 0 us
  waiting for transfers between devices: 29.4 us -> 24.5 us
  local copies, waits for them, and re-layouts: 3.49 us -> 2.01 us
    pallas_call x0 -> x6, Pallas kernels: none -> 26.2 us  [the longest x3 18.8 us: attend(): pl.pallas_call(functools.partial(attend_kernel, keys, (slots, heads, pool...]
    ppermute x0 -> x16, waiting for transfers between devices: none -> 24.5 us  [swap(): return lax.ppermute(array, 'pool', [(p, p ^ k) for p in range(pool)])]
    ppermute x0 -> x16, starting transfers between devices: none -> 18.2 us  [swap(): return lax.ppermute(array, 'pool', [(p, p ^ k) for p in range(pool)])]
    all_to_all x1 -> x0, waiting for transfers between devices: 15.8 us -> none  [on_device(): lax.all_to_all(outgoing, 'pool', split_axis=0, concat_axis=0, tiled=True)]
    all_gather x1 -> x0, waiting for transfers between devices: 13 us -> none  [on_device(): arrived = lax.all_gather(new_kv, 'pool', axis=0, tiled=True)]
    all_to_all x1 -> x0, starting transfers between devices: 7.55 us -> none  [on_device(): lax.all_to_all(outgoing, 'pool', split_axis=0, concat_axis=0, tiled=True)]
    dot_general x8 -> x0, matrix products: 4.96 us -> none  [the longest x4 3.33 us: fold_keys(): jnp.einsum('tgk,kd->tgd', weights.astype(jnp.bfloat16), values, preferred...]
    reduce_sum x6 -> x0, other arithmetic: 3.38 us -> none  [the longest x4 1.92 us: fold_keys(): totals = totals * factor + jnp.sum(weights, axis=2)]
  transfers between devices with their start and end apart: 2 -> 16, of which waited for: 2 -> 6; matrix products, arithmetic and copies ran while one was open for 17% -> 0% of each run, Pallas kernels for 0% -> 25%
where the time goes in v1:
time: 73.1 us; the launch traced here: 71.8 us
  Pallas kernels  26.2 us (36%)
  waiting for transfers between devices  24.5 us (34%)
  starting transfers between devices  18.2 us (25%)
  local copies, waits for them, and re-layouts  2.01 us (3%)
  between operations  0.86 us (1%)
    ppermute x16, waiting for transfers between devices, swap(): return lax.ppermute(array, 'pool', [(p, p ^ k) for p in range(pool)])  24.5 us
    pallas_call x3, Pallas kernels, attend(): pl.pallas_call(functools.partial(attend_kernel, keys, (slots, heads, pool...  18.8 us
    ppermute x16, starting transfers between devices, swap(): return lax.ppermute(array, 'pool', [(p, p ^ k) for p in range(pool)])  18.2 us
    pallas_call x1, Pallas kernels, pack_near(): pl.pallas_call(functools.partial(pack_near_kernel, near, (slots, heads, p...  2.95 us
    pallas_call x1, Pallas kernels, pack_far(): pl.pallas_call(functools.partial(pack_far_kernel, plan, (slots, heads, po...  2.77 us
    unnamed x38, local copies, waits for them, and re-layouts  2.01 us
    pallas_call x1, Pallas kernels, store_new(): pl.pallas_call(functools.partial(store_new_kernel, near, (heads, len(news...  1.68 us
  transfers between devices with their start and end apart: 16, of which 6 were waited for; matrix products, arithmetic and copies ran while one was open for 0% of the time, Pallas kernels for 25%

profile of v1, /device:TPU:0, one launch (start us, length us, event | category | flops | bytes accessed | tf_op | source)
XLA Modules:
  0.0 71.8 jit_solution(3673916561914005354)
XLA Ops:
  0.6 2.8 %pack_far.1 = (bf16[2,128,256]{2,1,0:T(8,128)(2,1)}, bf16[2,128,256]{2,1,0:T(8,128)(2,1)}, bf16[2,128,256]{2,1,0:T(8,128)(2,1)}, bf16[1,128,256]{2,1,0:T(8,128)(...) custom-call(s32[2,16]{1,0:T(2,128)} %hits_ref.9, s32[2]{0:T(128)} %blocks_ref.9, ...), custom_call_target="tpu_custom_call" | custom-call | tf_op jit(solution)/shard_map/pack_far/pallas_call | solution.py:69
  3.4 5.1 %collective-permute-start.2 = (bf16[2,128,256]{2,1,0:T(8,128)(2,1)}, bf16[2,128,256]{2,1,0:T(8,128)(2,1)S(1)}, u32[]{:S(2)}, u32[]{:S(2)}) collective-permute-start(bf16[2,128,256]{2,1,0:T(8,128)(2,1)} %get-tuple-element.21), channel_id=1, source_target_pairs={{0,12},{1,13},{2,14},{3,15},{4,8},{5,9},{6,10},{7,11},{8,4},{9,5},... | collective-permute-start | bytes 393224 | tf_op jit(solution)/shard_map/ppermute | solution.py:313
  8.6 1.2 %collective-permute-start.3 = (bf16[2,128,256]{2,1,0:T(8,128)(2,1)}, bf16[2,128,256]{2,1,0:T(8,128)(2,1)S(1)}, u32[]{:S(2)}, u32[]{:S(2)}) collective-permute-start(bf16[2,128,256]{2,1,0:T(8,128)(2,1)} %get-tuple-element.22), channel_id=1, source_target_pairs={{0,14},{1,15},{2,12},{3,13},{4,10},{5,11},{6,8},{7,9},{8,6},{9,7},... | collective-permute-start | bytes 393224 | tf_op jit(solution)/shard_map/ppermute | solution.py:313
  9.7 0.8 %collective-permute-start.4 = (bf16[2,128,256]{2,1,0:T(8,128)(2,1)}, bf16[2,128,256]{2,1,0:T(8,128)(2,1)S(1)}, u32[]{:S(2)}, u32[]{:S(2)}) collective-permute-start(bf16[2,128,256]{2,1,0:T(8,128)(2,1)} %get-tuple-element.23), channel_id=1, source_target_pairs={{0,8},{1,9},{2,10},{3,11},{4,12},{5,13},{6,14},{7,15},{8,0},{9,1},... | collective-permute-start | bytes 393224 | tf_op jit(solution)/shard_map/ppermute | solution.py:313
  10.5 2.1 %collective-permute-start.8 = (bf16[1,128,256]{2,1,0:T(8,128)(2,1)S(1)}, bf16[1,128,256]{2,1,0:T(8,128)(2,1)S(1)}, u32[]{:S(2)}, u32[]{:S(2)}) collective-permute-start(bf16[1,128,256]{2,1,0:T(8,128)(2,1)S(1)} %copy-done), channel_id=1, source_target_pairs={{0,8},{1,9},{2,10},{3,11},{4,12},{5,13},{6,14},{7,15},{8,0},{9,1},... | collective-permute-start | bytes 196616 | tf_op jit(solution)/shard_map/ppermute | solution.py:313
  12.7 15.6 %collective-permute-done.8.rest_1_ = bf16[1,128,256]{2,1,0:T(8,128)(2,1)S(1)} collective-permute-done((bf16[1,128,256]{2,1,0:T(8,128)(2,1)S(1)}, bf16[1,128,256]{2,1,0:T(8,128)(2,1)S(1)}, u32[]{:S(2)}, u32[]{:S(2)}) %collective-permute-start.8) | collective-permute-done | bytes 65568 | tf_op jit(solution)/shard_map/ppermute | solution.py:313
  28.3 0.6 copy-done.1
  28.9 3.0 %pack_near.1 = (bf16[2,128,256]{2,1,0:T(8,128)(2,1)}, bf16[2,128,256]{2,1,0:T(8,128)(2,1)}, bf16[2,128,256]{2,1,0:T(8,128)(2,1)}, bf16[2,128,256]{2,1,0:T(8,128)...) custom-call(s32[2,16]{1,0:T(2,128)} %hits_ref.9, s32[2]{0:T(128)} %blocks_ref.9, ...), custom_call_target="tpu_custom_call" | custom-call | tf_op jit(solution)/shard_map/pack_near/pallas_call | solution.py:129
  31.9 1.6 %collective-permute-start.10 = (bf16[2,128,256]{2,1,0:T(8,128)(2,1)}, bf16[2,128,256]{2,1,0:T(8,128)(2,1)S(1)}, u32[]{:S(2)}, u32[]{:S(2)}) collective-permute-start(bf16[2,128,256]{2,1,0:T(8,128)(2,1)} %get-tuple-element.26), channel_id=1, source_target_pairs={{0,2},{1,3},{2,0},{3,1},{4,6},{5,7},{6,4},{7,5},{8,10},{9,11},{10,... | collective-permute-start | bytes 393224 | tf_op jit(solution)/shard_map/ppermute | solution.py:313
  33.8 1.7 %collective-permute-start.13 = (bf16[2,128,256]{2,1,0:T(8,128)(2,1)}, bf16[2,128,256]{2,1,0:T(8,128)(2,1)S(1)}, u32[]{:S(2)}, u32[]{:S(2)}) collective-permute-start(bf16[2,128,256]{2,1,0:T(8,128)(2,1)} %get-tuple-element.29), channel_id=1, source_target_pairs={{0,5},{1,4},{2,7},{3,6},{4,1},{5,0},{6,3},{7,2},{8,13},{9,12},{10,... | collective-permute-start | bytes 393224 | tf_op jit(solution)/shard_map/ppermute | solution.py:313
  35.5 1.4 %collective-permute-start.14 = (bf16[2,128,256]{2,1,0:T(8,128)(2,1)}, bf16[2,128,256]{2,1,0:T(8,128)(2,1)S(1)}, u32[]{:S(2)}, u32[]{:S(2)}) collective-permute-start(bf16[2,128,256]{2,1,0:T(8,128)(2,1)} %get-tuple-element.30), channel_id=1, source_target_pairs={{0,6},{1,7},{2,4},{3,5},{4,2},{5,3},{6,0},{7,1},{8,14},{9,15},{10,... | collective-permute-start | bytes 393224 | tf_op jit(solution)/shard_map/ppermute | solution.py:313
  36.9 1.7 %collective-permute-done.10.rest_3_ = bf16[2,128,256]{2,1,0:T(8,128)(2,1)S(1)} collective-permute-done((bf16[2,128,256]{2,1,0:T(8,128)(2,1)}, bf16[2,128,256]{2,1,0:T(8,128)(2,1)S(1)}, u32[]{:S(2)}, u32[]{:S(2)}) %collective-permute-start.10) | collective-permute-done | bytes 131104 | tf_op jit(solution)/shard_map/ppermute | solution.py:313
  38.6 1.7 %collective-permute-done.11.rest_4_ = bf16[2,128,256]{2,1,0:T(8,128)(2,1)S(1)} collective-permute-done((bf16[2,128,256]{2,1,0:T(8,128)(2,1)}, bf16[2,128,256]{2,1,0:T(8,128)(2,1)S(1)}, u32[]{:S(2)}, u32[]{:S(2)}) %collective-permute-start.11) | collective-permute-done | bytes 131104 | tf_op jit(solution)/shard_map/ppermute | solution.py:313
  40.3 0.7 collective-permute-start.5
  41.1 0.9 %collective-permute-done.13.rest_6_ = bf16[2,128,256]{2,1,0:T(8,128)(2,1)S(1)} collective-permute-done((bf16[2,128,256]{2,1,0:T(8,128)(2,1)}, bf16[2,128,256]{2,1,0:T(8,128)(2,1)S(1)}, u32[]{:S(2)}, u32[]{:S(2)}) %collective-permute-start.13) | collective-permute-done | bytes 131104 | tf_op jit(solution)/shard_map/ppermute | solution.py:313
  42.0 1.0 %collective-permute-start.7 = (bf16[2,128,256]{2,1,0:T(8,128)(2,1)S(1)}, bf16[2,128,256]{2,1,0:T(8,128)(2,1)S(1)}, u32[]{:S(2)}, u32[]{:S(2)}) collective-permute-start(bf16[2,128,256]{2,1,0:T(8,128)(2,1)S(1)} %collective-permute-done.4.rest_2_), channel_id=1, source_target_pairs={{0,1},{1,0},{2,3},{3,2},{4,5},{5,4},{6,7},{7,6},{8,9},{9,8},{10,11... | collective-permute-start | bytes 393224 | tf_op jit(solution)/shard_map/ppermute | solution.py:313
  43.0 3.9 %collective-permute-done.14.rest_7_ = bf16[2,128,256]{2,1,0:T(8,128)(2,1)S(1)} collective-permute-done((bf16[2,128,256]{2,1,0:T(8,128)(2,1)}, bf16[2,128,256]{2,1,0:T(8,128)(2,1)S(1)}, u32[]{:S(2)}, u32[]{:S(2)}) %collective-permute-start.14) | collective-permute-done | bytes 131104 | tf_op jit(solution)/shard_map/ppermute | solution.py:313
  47.0 1.0 %collective-permute-start = (bf16[1,128,256]{2,1,0:T(8,128)(2,1)S(1)}, bf16[1,128,256]{2,1,0:T(8,128)(2,1)S(1)}, u32[]{:S(2)}, u32[]{:S(2)}) collective-permute-start(bf16[1,128,256]{2,1,0:T(8,128)(2,1)S(1)} %copy-done.18), channel_id=1, source_target_pairs={{0,10},{1,11},{2,8},{3,9},{4,14},{5,15},{6,12},{7,13},{8,2},{9,3},... | collective-permute-start | bytes 196616 | tf_op jit(solution)/shard_map/ppermute | solution.py:313
  47.9 0.6 collective-permute-done.15.rest_8_
  48.5 1.3 %collective-permute-start.1 = (bf16[1,128,256]{2,1,0:T(8,128)(2,1)S(1)}, bf16[1,128,256]{2,1,0:T(8,128)(2,1)S(1)}, u32[]{:S(2)}, u32[]{:S(2)}) collective-permute-start(bf16[1,128,256]{2,1,0:T(8,128)(2,1)S(1)} %copy-done.17), channel_id=1, source_target_pairs={{0,11},{1,10},{2,9},{3,8},{4,15},{5,14},{6,13},{7,12},{8,3},{9,2},... | collective-permute-start | bytes 196616 | tf_op jit(solution)/shard_map/ppermute | solution.py:313
  49.9 6.4 %shard_map.77 = (f32[1024,128]{1,0:T(8,128)}, f32[1024,128]{1,0:T(8,128)}) custom-call(s32[2,16]{1,0:T(2,128)} %hits_ref.9, s32[2]{0:T(128)} %blocks_ref.9, bf16[1,128,1024]{2,1,0:T(8,128)(2,1)} %query_ref.5, bf16[1,128,256]{2,1,0:T(8,128)(2,1)} %rest_0_.5, bf16[1,128,256]{2,1,0:T(8,128)(2,1)} %get-tuple-element.24.rest_1_, bf16[2,128,256]{2,1,0:T(8,128)(2,1)} %copy-done.8, ...), custom_call_target="tpu_custom_call" | custom-call | flops 603979776 | bytes 1048576 | tf_op jit(solution)/shard_map/pallas_call | solution.py:288
  56.3 1.7 %store_new.1 = bf16[1,8,128,256]{3,2,1,0:T(8,128)(2,1)} custom-call(s32[2,2]{1,0:T(2,128)} %owners_ref.3, bf16[1,128,256]{2,1,0:T(8,128)(2,1)} %rest_0_.5, bf16[1,128,256]{2,1,0:T(8,128)(2,1)} %copy-done.1, bf16[2,128,256]{2,1,0:T(8,128)(2,1)} %copy-done.8, bf16[2,128,256]{2,1,0:T(8,128)(2,1)} %copy-done.9, bf16[2,128,256]{2,1,0:T(8,128)(2,1)} %copy-done.10, ...), custom_call_target="tpu_custom_call" | custom-call | tf_op jit(solution)/shard_map/store_new/pallas_call | solution.py:187
  58.7 6.7 %shard_map.78 = (f32[1024,128]{1,0:T(8,128)}, f32[1024,128]{1,0:T(8,128)}) custom-call(s32[2,16]{1,0:T(2,128)} %hits_ref.9, s32[2]{0:T(128)} %blocks_ref.9, bf16[1,128,1024]{2,1,0:T(8,128)(2,1)} %query_ref.5, bf16[2,128,256]{2,1,0:T(8,128)(2,1)} %copy-done.2, bf16[2,128,256]{2,1,0:T(8,128)(2,1)} %copy-done.3, bf16[2,128,256]{2,1,0:T(8,128)(2,1)} %copy-done.4, ...), custom_call_target="tpu_custom_call" | custom-call | flops 402653184 | bytes 1048576 | tf_op jit(solution)/shard_map/pallas_call | solution.py:288
  66.0 5.8 %shard_map.79 = bf16[1,128,1024]{2,1,0:T(8,128)(2,1)} custom-call(s32[2,16]{1,0:T(2,128)} %hits_ref.9, s32[2]{0:T(128)} %blocks_ref.9, bf16[1,128,1024]{2,1,0:T(8,128)(2,1)} %query_ref.5, bf16[1,128,256]{2,1,0:T(8,128)(2,1)} %copy-done.15, bf16[1,128,256]{2,1,0:T(8,128)(2,1)} %copy-done.16, f32[1024,128]{1,0:T(8,128)} %get-tuple-element.34.rest_2_, ...), custom_call_target="tpu_custom_call" | custom-call | flops 134217728 | bytes 1048576 | tf_op jit(solution)/shard_map/pallas_call | solution.py:288
  (52 shorter events, 1.8 us)
Async XLA Ops:
  0.6 9.9 %copy-start = (bf16[1,128,256]{2,1,0:T(8,128)(2,1)S(1)}, bf16[1,128,256]{2,1,0:T(8,128)(2,1)}, u32[]{:S(2)}) copy-start(bf16[1,128,256]{2,1,0:T(8,128)(2,1)} %rest_0_.5) | copy-start | bytes 196612
  3.4 30.1 %collective-permute-start.2 = (bf16[2,128,256]{2,1,0:T(8,128)(2,1)}, bf16[2,128,256]{2,1,0:T(8,128)(2,1)S(1)}, u32[]{:S(2)}, u32[]{:S(2)}) collective-permute-start(bf16[2,128,256]{2,1,0:T(8,128)(2,1)} %get-tuple-element.21), channel_id=1, source_target_pairs={{0,12},{1,13},{2,14},{3,15},{4,8},{5,9},{6,10},{7,11},{8,4},{9,5},... | collective-permute-start | bytes 393224 | tf_op jit(solution)/shard_map/ppermute | solution.py:313
  8.6 25.2 %collective-permute-start.3 = (bf16[2,128,256]{2,1,0:T(8,128)(2,1)}, bf16[2,128,256]{2,1,0:T(8,128)(2,1)S(1)}, u32[]{:S(2)}, u32[]{:S(2)}) collective-permute-start(bf16[2,128,256]{2,1,0:T(8,128)(2,1)} %get-tuple-element.22), channel_id=1, source_target_pairs={{0,14},{1,15},{2,12},{3,13},{4,10},{5,11},{6,8},{7,9},{8,6},{9,7},... | collective-permute-start | bytes 393224 | tf_op jit(solution)/shard_map/ppermute | solution.py:313
  9.7 37.2 %copy-start.18 = (bf16[1,128,256]{2,1,0:T(8,128)(2,1)S(1)}, bf16[1,128,256]{2,1,0:T(8,128)(2,1)}, u32[]{:S(2)}) copy-start(bf16[1,128,256]{2,1,0:T(8,128)(2,1)} %get-tuple-element.19) | copy-start | bytes 196612
  9.7 38.8 %copy-start.17 = (bf16[1,128,256]{2,1,0:T(8,128)(2,1)S(1)}, bf16[1,128,256]{2,1,0:T(8,128)(2,1)}, u32[]{:S(2)}) copy-start(bf16[1,128,256]{2,1,0:T(8,128)(2,1)} %get-tuple-element.20) | copy-start | bytes 196612
  9.7 24.1 %collective-permute-start.4 = (bf16[2,128,256]{2,1,0:T(8,128)(2,1)}, bf16[2,128,256]{2,1,0:T(8,128)(2,1)S(1)}, u32[]{:S(2)}, u32[]{:S(2)}) collective-permute-start(bf16[2,128,256]{2,1,0:T(8,128)(2,1)} %get-tuple-element.23), channel_id=1, source_target_pairs={{0,8},{1,9},{2,10},{3,11},{4,12},{5,13},{6,14},{7,15},{8,0},{9,1},... | collective-permute-start | bytes 393224 | tf_op jit(solution)/shard_map/ppermute | solution.py:313
  10.5 17.7 %collective-permute-start.8 = (bf16[1,128,256]{2,1,0:T(8,128)(2,1)S(1)}, bf16[1,128,256]{2,1,0:T(8,128)(2,1)S(1)}, u32[]{:S(2)}, u32[]{:S(2)}) collective-permute-start(bf16[1,128,256]{2,1,0:T(8,128)(2,1)S(1)} %copy-done), channel_id=1, source_target_pairs={{0,8},{1,9},{2,10},{3,11},{4,12},{5,13},{6,14},{7,15},{8,0},{9,1},... | collective-permute-start | bytes 196616 | tf_op jit(solution)/shard_map/ppermute | solution.py:313
  31.9 3.7 %collective-permute-start.9 = (bf16[2,128,256]{2,1,0:T(8,128)(2,1)}, bf16[2,128,256]{2,1,0:T(8,128)(2,1)S(1)}, u32[]{:S(2)}, u32[]{:S(2)}) collective-permute-start(bf16[2,128,256]{2,1,0:T(8,128)(2,1)} %get-tuple-element.25), channel_id=1, source_target_pairs={{0,1},{1,0},{2,3},{3,2},{4,5},{5,4},{6,7},{7,6},{8,9},{9,8},{10,11... | collective-permute-start | bytes 393224 | tf_op jit(solution)/shard_map/ppermute | solution.py:313
  31.9 6.6 %collective-permute-start.10 = (bf16[2,128,256]{2,1,0:T(8,128)(2,1)}, bf16[2,128,256]{2,1,0:T(8,128)(2,1)S(1)}, u32[]{:S(2)}, u32[]{:S(2)}) collective-permute-start(bf16[2,128,256]{2,1,0:T(8,128)(2,1)} %get-tuple-element.26), channel_id=1, source_target_pairs={{0,2},{1,3},{2,0},{3,1},{4,6},{5,7},{6,4},{7,5},{8,10},{9,11},{10,... | collective-permute-start | bytes 393224 | tf_op jit(solution)/shard_map/ppermute | solution.py:313
  33.5 22.7 %copy-start.2 = (bf16[2,128,256]{2,1,0:T(8,128)(2,1)}, bf16[2,128,256]{2,1,0:T(8,128)(2,1)S(1)}, u32[]{:S(2)}) copy-start(bf16[2,128,256]{2,1,0:T(8,128)(2,1)S(1)} %collective-permute-done.2.rest_0_) | copy-start | bytes 393220
  33.5 6.8 %collective-permute-start.11 = (bf16[2,128,256]{2,1,0:T(8,128)(2,1)}, bf16[2,128,256]{2,1,0:T(8,128)(2,1)S(1)}, u32[]{:S(2)}, u32[]{:S(2)}) collective-permute-start(bf16[2,128,256]{2,1,0:T(8,128)(2,1)} %get-tuple-element.27), channel_id=1, source_target_pairs={{0,3},{1,2},{2,1},{3,0},{4,7},{5,6},{6,5},{7,4},{8,11},{9,10},{10,... | collective-permute-start | bytes 393224 | tf_op jit(solution)/shard_map/ppermute | solution.py:313
  33.8 22.5 %copy-start.3 = (bf16[2,128,256]{2,1,0:T(8,128)(2,1)}, bf16[2,128,256]{2,1,0:T(8,128)(2,1)S(1)}, u32[]{:S(2)}) copy-start(bf16[2,128,256]{2,1,0:T(8,128)(2,1)S(1)} %collective-permute-done.3.rest_1_) | copy-start | bytes 393220
  33.8 7.2 %collective-permute-start.12 = (bf16[2,128,256]{2,1,0:T(8,128)(2,1)}, bf16[2,128,256]{2,1,0:T(8,128)(2,1)S(1)}, u32[]{:S(2)}, u32[]{:S(2)}) collective-permute-start(bf16[2,128,256]{2,1,0:T(8,128)(2,1)} %get-tuple-element.28), channel_id=1, source_target_pairs={{0,4},{1,5},{2,6},{3,7},{4,0},{5,1},{6,2},{7,3},{8,12},{9,13},{10,... | collective-permute-start | bytes 393224 | tf_op jit(solution)/shard_map/ppermute | solution.py:313
  33.8 22.4 %copy-start.4 = (bf16[2,128,256]{2,1,0:T(8,128)(2,1)}, bf16[2,128,256]{2,1,0:T(8,128)(2,1)S(1)}, u32[]{:S(2)}) copy-start(bf16[2,128,256]{2,1,0:T(8,128)(2,1)S(1)} %collective-permute-done.4.rest_2_) | copy-start | bytes 393220
  33.8 8.1 %collective-permute-start.13 = (bf16[2,128,256]{2,1,0:T(8,128)(2,1)}, bf16[2,128,256]{2,1,0:T(8,128)(2,1)S(1)}, u32[]{:S(2)}, u32[]{:S(2)}) collective-permute-start(bf16[2,128,256]{2,1,0:T(8,128)(2,1)} %get-tuple-element.29), channel_id=1, source_target_pairs={{0,5},{1,4},{2,7},{3,6},{4,1},{5,0},{6,3},{7,2},{8,13},{9,12},{10,... | collective-permute-start | bytes 393224 | tf_op jit(solution)/shard_map/ppermute | solution.py:313
  35.5 14.3 %copy-start.8 = (bf16[2,128,256]{2,1,0:T(8,128)(2,1)}, bf16[2,128,256]{2,1,0:T(8,128)(2,1)S(1)}, u32[]{:S(2)}) copy-start(bf16[2,128,256]{2,1,0:T(8,128)(2,1)S(1)} %collective-permute-done.9.rest_2_) | copy-start | bytes 393220
  35.5 11.4 %collective-permute-start.14 = (bf16[2,128,256]{2,1,0:T(8,128)(2,1)}, bf16[2,128,256]{2,1,0:T(8,128)(2,1)S(1)}, u32[]{:S(2)}, u32[]{:S(2)}) collective-permute-start(bf16[2,128,256]{2,1,0:T(8,128)(2,1)} %get-tuple-element.30), channel_id=1, source_target_pairs={{0,6},{1,7},{2,4},{3,5},{4,2},{5,3},{6,0},{7,1},{8,14},{9,15},{10,... | collective-permute-start | bytes 393224 | tf_op jit(solution)/shard_map/ppermute | solution.py:313
  38.6 11.2 %copy-start.9 = (bf16[2,128,256]{2,1,0:T(8,128)(2,1)}, bf16[2,128,256]{2,1,0:T(8,128)(2,1)S(1)}, u32[]{:S(2)}) copy-start(bf16[2,128,256]{2,1,0:T(8,128)(2,1)S(1)} %collective-permute-done.10.rest_3_) | copy-start | bytes 393220
  38.6 9.9 %collective-permute-start.15 = (bf16[2,128,256]{2,1,0:T(8,128)(2,1)}, bf16[2,128,256]{2,1,0:T(8,128)(2,1)S(1)}, u32[]{:S(2)}, u32[]{:S(2)}) collective-permute-start(bf16[2,128,256]{2,1,0:T(8,128)(2,1)} %get-tuple-element.31), channel_id=1, source_target_pairs={{0,7},{1,6},{2,5},{3,4},{4,3},{5,2},{6,1},{7,0},{8,15},{9,14},{10,... | collective-permute-start | bytes 393224 | tf_op jit(solution)/shard_map/ppermute | solution.py:313
  40.3 17.6 %collective-permute-start.5 = (bf16[2,128,256]{2,1,0:T(8,128)(2,1)S(1)}, bf16[2,128,256]{2,1,0:T(8,128)(2,1)S(1)}, u32[]{:S(2)}, u32[]{:S(2)}) collective-permute-start(bf16[2,128,256]{2,1,0:T(8,128)(2,1)S(1)} %collective-permute-done.2.rest_0_), channel_id=1, source_target_pairs={{0,1},{1,0},{2,3},{3,2},{4,5},{5,4},{6,7},{7,6},{8,9},{9,8},{10,11... | collective-permute-start | bytes 393224 | tf_op jit(solution)/shard_map/ppermute | solution.py:313
  41.0 17.0 %collective-permute-start.6 = (bf16[2,128,256]{2,1,0:T(8,128)(2,1)S(1)}, bf16[2,128,256]{2,1,0:T(8,128)(2,1)S(1)}, u32[]{:S(2)}, u32[]{:S(2)}) collective-permute-start(bf16[2,128,256]{2,1,0:T(8,128)(2,1)S(1)} %collective-permute-done.3.rest_1_), channel_id=1, source_target_pairs={{0,1},{1,0},{2,3},{3,2},{4,5},{5,4},{6,7},{7,6},{8,9},{9,8},{10,11... | collective-permute-start | bytes 393224 | tf_op jit(solution)/shard_map/ppermute | solution.py:313
  42.0 16.0 %collective-permute-start.7 = (bf16[2,128,256]{2,1,0:T(8,128)(2,1)S(1)}, bf16[2,128,256]{2,1,0:T(8,128)(2,1)S(1)}, u32[]{:S(2)}, u32[]{:S(2)}) collective-permute-start(bf16[2,128,256]{2,1,0:T(8,128)(2,1)S(1)} %collective-permute-done.4.rest_2_), channel_id=1, source_target_pairs={{0,1},{1,0},{2,3},{3,2},{4,5},{5,4},{6,7},{7,6},{8,9},{9,8},{10,11... | collective-permute-start | bytes 393224 | tf_op jit(solution)/shard_map/ppermute | solution.py:313
  47.0 18.4 %collective-permute-start = (bf16[1,128,256]{2,1,0:T(8,128)(2,1)S(1)}, bf16[1,128,256]{2,1,0:T(8,128)(2,1)S(1)}, u32[]{:S(2)}, u32[]{:S(2)}) collective-permute-start(bf16[1,128,256]{2,1,0:T(8,128)(2,1)S(1)} %copy-done.18), channel_id=1, source_target_pairs={{0,10},{1,11},{2,8},{3,9},{4,14},{5,15},{6,12},{7,13},{8,2},{9,3},... | collective-permute-start | bytes 196616 | tf_op jit(solution)/shard_map/ppermute | solution.py:313
  48.5 16.9 %collective-permute-start.1 = (bf16[1,128,256]{2,1,0:T(8,128)(2,1)S(1)}, bf16[1,128,256]{2,1,0:T(8,128)(2,1)S(1)}, u32[]{:S(2)}, u32[]{:S(2)}) collective-permute-start(bf16[1,128,256]{2,1,0:T(8,128)(2,1)S(1)} %copy-done.17), channel_id=1, source_target_pairs={{0,11},{1,10},{2,9},{3,8},{4,15},{5,14},{6,13},{7,12},{8,3},{9,2},... | collective-permute-start | bytes 196616 | tf_op jit(solution)/shard_map/ppermute | solution.py:313
  (11 other events, 34.4 us)

commit v2 on v0

v2 whole, which is shorter than its diff:
```python
import functools
import math

import jax
import jax.numpy as jnp
from jax import lax
from jax.experimental import pallas as pl
from jax.experimental.pallas import tpu as pltpu
from jax.sharding import PartitionSpec as P

MINUS_BIG = -1e30
CHUNK = 8
HBM = pl.BlockSpec(memory_space=pltpu.HBM)
VMEM = pl.BlockSpec(memory_space=pltpu.VMEM)
SMEM = pl.BlockSpec(memory_space=pltpu.SMEM)
GRANT = pltpu.CompilerParams(vmem_limit_bytes=16 << 20)


def owner_position(hits_ref, request, owner, slots, pool):
    first = hits_ref[request, 0] // slots
    return lax.rem(owner - first + pool, pool)


def held_slot(hits_ref, blocks_ref, request, me, slots, pool):
    position = owner_position(hits_ref, request, me, slots, pool)
    longest = hits_ref.shape[1]
    entry = hits_ref[request, jnp.minimum(position, longest - 1)]
    return jnp.where(position < blocks_ref[request], lax.rem(entry, slots), 0)


def wanted_request(owners_ref, device):
    found = jnp.int32(0)
    any_found = jnp.bool_(False)
    for request in range(owners_ref.shape[0]):
        for copy in range(owners_ref.shape[1]):
            hit = owners_ref[request, copy] == device
            found = jnp.where(hit, request, found)
            any_found = jnp.logical_or(any_found, hit)
    return found, any_found


def pack_kernel(plan, sizes, hits_ref, blocks_ref, pool_ref, new_ref, *rest):
    slots, heads, pool = sizes
    outs, (sems,) = rest[: len(plan)], rest[len(plan) :]
    me = lax.axis_index("pool")
    loads = []
    for index, targets in enumerate(plan):
        for place, k in enumerate(targets):
            if k is None:
                source = new_ref.at[0]
            else:
                other = lax.bitwise_xor(me, k)
                slot = held_slot(hits_ref, blocks_ref, other // heads, me, slots, pool)
                source = pool_ref.at[slot, lax.rem(other, heads)]
            load = pltpu.make_async_copy(source, outs[index].at[place], sems.at[len(loads)])
            load.start()
            loads.append(load)
    for load in loads:
        load.wait()


def pack(plan, hits, blocks, pool_kv, new_kv, pool):
    slots, heads, length, width = pool_kv.shape
    rows = sum(len(targets) for targets in plan)
    return pl.pallas_call(
        functools.partial(pack_kernel, plan, (slots, heads, pool)),
        out_shape=[
            jax.ShapeDtypeStruct((len(targets), length, width), pool_kv.dtype) for targets in plan
        ],
        in_specs=[SMEM, SMEM, HBM, HBM],
        out_specs=[VMEM] * len(plan),
        scratch_shapes=[pltpu.SemaphoreType.DMA((rows,))],
        compiler_params=GRANT,
        name="pack",
    )(hits, blocks, pool_kv, new_kv)


def pick(refs, which, store):
    for m, (ref, place) in enumerate(refs):
        @pl.when(which == m)
        def _(ref=ref, place=place):
            store(ref[place])


def route_kernel(late, sizes, owners_ref, cached_ref, *rest):
    heads, requests = sizes
    mine_refs = [(ref, 0) for ref in rest[:requests]]
    over_refs = [(rest[requests], 1)] + [(ref, 0) for ref in rest[requests + 1 : 2 * requests]]
    outs = rest[2 * requests :]
    me = lax.axis_index("pool")
    for index, k in enumerate(late):
        wanted, _ = wanted_request(owners_ref, lax.bitwise_xor(me, k))
        which = lax.bitwise_xor(wanted, me // heads)
        outs[index][0] = cached_ref[index]

        def store_mine(value, index=index):
            outs[index][1] = value

        def store_over(value, index=index):
            outs[index][2] = value

        pick(mine_refs, which, store_mine)
        pick(over_refs, which, store_over)


def route(late, owners, cached, mine, over, heads):
    _, length, width = cached.shape
    return pl.pallas_call(
        functools.partial(route_kernel, late, (heads, len(mine))),
        out_shape=[jax.ShapeDtypeStruct((3, length, width), cached.dtype)] * len(late),
        in_specs=[SMEM] + [VMEM] * (1 + len(mine) + len(over)),
        out_specs=[VMEM] * len(late),
        compiler_params=GRANT,
        name="route",
    )(owners, cached, *mine, *over)


def store_kernel(late, half, sizes, owners_ref, *rest):
    heads, requests = sizes
    mine_refs = [(ref, 0) for ref in rest[:requests]]
    over_refs = [(rest[requests], 1)] + [(ref, 0) for ref in rest[requests + 1 : 2 * requests]]
    pieces, out_ref = rest[2 * requests : -1], rest[-1]
    me = lax.axis_index("pool")
    head = lax.rem(me, heads)
    wanted, owned = wanted_request(owners_ref, me)
    which = lax.bitwise_xor(wanted, me // heads)

    @pl.when(owned)
    def _():
        def store_mine(value):
            out_ref[0, head] = value

        def store_over(value):
            out_ref[0, lax.bitwise_xor(head, half)] = value

        pick(mine_refs, which, store_mine)
        pick(over_refs, which, store_over)
        for piece, k in zip(pieces, late):
            out_ref[0, lax.bitwise_xor(head, k)] = piece[1]
            out_ref[0, lax.bitwise_xor(head, k ^ half)] = piece[2]

    @pl.when(jnp.logical_not(owned))
    def _():
        out_ref[...] = jnp.zeros_like(out_ref)


def store(late, half, owners, mine, over, pieces, heads):
    _, length, width = mine[0].shape
    return pl.pallas_call(
        functools.partial(store_kernel, late, half, (heads, len(mine))),
        out_shape=jax.ShapeDtypeStruct((1, heads, length, width), mine[0].dtype),
        in_specs=[SMEM] + [VMEM] * (len(mine) + len(over) + len(pieces)),
        out_specs=VMEM,
        compiler_params=GRANT,
        name="store",
    )(owners, *mine, *over, *pieces)


def attend_kernel(keys, sizes, first, last, hits_ref, blocks_ref, query_ref, *rest):
    slots, heads, pool, arrays = sizes
    kv_refs, rest = rest[:arrays], rest[arrays:]
    if not first:
        (acc_in, stat_in), rest = rest[:2], rest[2:]
    if last:
        (out_ref,), rest = rest[:1], rest[1:]
    else:
        (acc_out, stat_out), rest = rest[:2], rest[2:]
    (values_ref,) = rest
    me = lax.axis_index("pool")
    request = me // heads
    length = query_ref.shape[1]
    head_dim = values_ref.shape[0]
    groups = query_ref.shape[2] // head_dim
    step = 2 if groups % 2 == 0 else 1
    columns = step * length
    to_exponent = math.log2(math.e) / math.sqrt(head_dim)
    alive = []
    for index, (k, array, place) in enumerate(keys):
        values = kv_refs[array][place, :, head_dim:]
        values_ref[:, index * length : (index + 1) * length] = values.T
        if k is None:
            key_at = lax.broadcasted_iota(jnp.int32, (length, columns), 0)
            token_at = lax.rem(lax.broadcasted_iota(jnp.int32, (length, columns), 1), length)
            alive.append(key_at <= token_at)
        else:
            position = owner_position(hits_ref, request, lax.bitwise_xor(me, k), slots, pool)
            alive.append(position < blocks_ref[request])
    for group in range(0, groups, step):
        at = slice(group * length, (group + step) * length)
        query = jnp.concatenate(
            [query_ref[0, :, h * head_dim : (h + 1) * head_dim] for h in range(group, group + step)],
            0,
        )
        parts = []
        for live, (_k, array, place) in zip(alive, keys):
            scores = lax.dot_general(
                kv_refs[array][place, :, :head_dim],
                query,
                (((1,), (1,)), ((), ())),
                preferred_element_type=jnp.float32,
            )
            parts.append(jnp.where(live, scores, MINUS_BIG))
        top = jnp.max(functools.reduce(jnp.maximum, parts), axis=0, keepdims=True)
        if not first:
            old_top = stat_in[0:1, at]
            top = jnp.maximum(top, old_top)
            factor = jnp.exp2((old_top - top) * to_exponent)
        weights = [jnp.exp2((part - top) * to_exponent) for part in parts]
        total = jnp.sum(functools.reduce(jnp.add, weights), axis=0, keepdims=True)
        mixed = jnp.dot(
            values_ref[...],
            jnp.concatenate([part.astype(jnp.bfloat16) for part in weights], 0),
            preferred_element_type=jnp.float32,
        )
        if not first:
            total = total + stat_in[1:2, at] * factor
            mixed = mixed + acc_in[:, at] * factor
        if last:
            mixed = mixed * (1.0 / total)
            for place, h in enumerate(range(group, group + step)):
                out_ref[0, :, h * head_dim : (h + 1) * head_dim] = mixed[
                    :, place * length : (place + 1) * length
                ].T.astype(out_ref.dtype)
        else:
            acc_out[:, at] = mixed
            stat_out[0:1, at] = top
            stat_out[1:2, at] = total


def attend(keys, hits, blocks, queries, arrays, state, last, slots, heads, pool):
    _, length, columns = queries.shape
    width = arrays[0].shape[-1]
    head_dim = width // 2
    rows = columns // head_dim * length
    first = state is None
    scores = rows * len(keys) * length
    return pl.pallas_call(
        functools.partial(attend_kernel, keys, (slots, heads, pool, len(arrays)), first, last),
        out_shape=jax.ShapeDtypeStruct(queries.shape, queries.dtype)
        if last
        else (
            jax.ShapeDtypeStruct((head_dim, rows), jnp.float32),
            jax.ShapeDtypeStruct((8, rows), jnp.float32),
        ),
        in_specs=[SMEM, SMEM] + [VMEM] * (1 + len(arrays) + (0 if first else 2)),
        out_specs=VMEM if last else (VMEM, VMEM),
        scratch_shapes=[pltpu.VMEM((head_dim, len(keys) * length), jnp.bfloat16)],
        cost_estimate=pl.CostEstimate(
            flops=4 * scores * head_dim,
            bytes_accessed=4 * rows * width,
            transcendentals=scores,
        ),
        compiler_params=GRANT,
    )(hits, blocks, queries, *arrays, *(() if first else state))


def layout(pool, heads):
    far = list(range(heads, pool, 2))
    far = far[len(far) // 2 :] + far[: len(far) // 2]
    half = heads // 2
    return far[:-1], [far[-1], far[-1] ^ 1], list(range(half, heads)), list(range(1, half))


def on_device(pool, queries, new_kv, pool_kv, hits, blocks, owners):
    slots, heads, _, _ = pool_kv.shape
    requests = hits.shape[0]
    far_pairs, far_last, early, late = layout(pool, heads)
    half = heads // 2

    def swap(k, array):
        return lax.ppermute(array, "pool", [(p, p ^ k) for p in range(pool)])

    mine = [new_kv] + [swap(m * heads, new_kv) for m in range(1, requests)]
    plan = [(k, k ^ 1) for k in far_pairs] + [(k,) for k in far_last]
    plan += [(k, None) if k == half else (k,) for k in early] + [(0,), tuple(late)]
    packed = pack(plan, hits, blocks, pool_kv, new_kv, pool)
    own, cached = packed[-2:]
    moved = {}
    for targets, array in zip(plan[:-2], packed):
        moved[targets[0]] = swap(targets[0], array)
    over = [moved[half]] + [swap(half, mine[m]) for m in range(1, requests)]
    routed = route(late, owners, cached, mine, over, heads)
    for k, array in zip(late, routed):
        moved[k] = swap(k, array)
    mates = {k: swap(1, moved[k]) for k in far_pairs}

    near = [(None, new_kv, 0), (0, own, 0)] + [(k, moved[k], 0) for k in early]
    rest = [(k, moved[k], 0) for k in late]
    for k in far_pairs:
        rest += [(k, moved[k], 0), (k ^ 1, mates[k], 1)]
    chunks = [near] + [rest[i : i + CHUNK] for i in range(0, len(rest), CHUNK)]
    chunks += [[(k, moved[k], 0) for k in far_last]]
    state = None
    for number, chunk in enumerate(chunks):
        state = attend(
            [(k, i, place) for i, (k, _, place) in enumerate(chunk)],
            hits, blocks, queries, [array for _, array, _ in chunk], state,
            number == len(chunks) - 1, slots, heads, pool,
        )
    new_store = store(late, half, owners, mine, over, [moved[k] for k in late], heads)
    return state, new_store


def solution(mesh):
    pool = mesh.shape["pool"]
    placed = (
        P(("grp", "pool"), None, None),
        P(("grp", "pool"), None, None),
        P(("grp", "pool"), None, None, None),
        P("grp", None),
        P("grp"),
        P("grp", None),
    )

    def whole(queries, new_kv, pool_kv, hits, blocks, owners):
        step = jax.shard_map(
            functools.partial(on_device, pool),
            mesh=mesh,
            in_specs=placed,
            out_specs=(P(("grp", "pool"), None, None), P(("grp", "pool"), None, None, None)),
            check_vma=False,
        )
        return step(queries, new_kv, pool_kv, hits, blocks, owners)

    return whole
```

time: 75.3 us -> 52.7 us (0.70)
  the two profiles are of different devices: /device:TPU:0 before, /device:TPU:1 now
where the time goes in v2:
time: 52.7 us; the launch traced here: 52.5 us
  starting transfers between devices  28.2 us (54%)
  Pallas kernels  14 us (27%)
  waiting for transfers between devices  6.06 us (11%)
  local copies, waits for them, and re-layouts  3.41 us (6%)
  between operations  0.73 us (1%)
    ppermute x17, starting transfers between devices, swap(): return lax.ppermute(array, 'pool', [(p, p ^ k) for p in range(pool)])  28.2 us
    pallas_call x4, Pallas kernels, attend(): pl.pallas_call(functools.partial(attend_kernel, keys, (slots, heads, pool...  9.24 us
    ppermute x17, waiting for transfers between devices, swap(): return lax.ppermute(array, 'pool', [(p, p ^ k) for p in range(pool)])  6.06 us
    unnamed x14, local copies, waits for them, and re-layouts  3.41 us
    pallas_call x1, Pallas kernels, pack(): pl.pallas_call(functools.partial(pack_kernel, plan, (slots, heads, pool))...  2.76 us
    pallas_call x1, Pallas kernels, store(): pl.pallas_call(functools.partial(store_kernel, late, half, (heads, len(mi...  1.4 us
  transfers between devices with their start and end apart: 17, of which 5 were waited for; matrix products, arithmetic and copies ran while one was open for 0% of the time, Pallas kernels for 22%

profile of v2, /device:TPU:1, one launch (start us, length us, event | category | flops | bytes accessed | tf_op | source)
XLA Modules:
  0.0 52.5 jit_solution(5307167796013033262)
XLA Ops:
  0.6 3.2 %collective-permute-start.4 = (bf16[1,128,256]{2,1,0:T(8,128)(2,1)}, bf16[1,128,256]{2,1,0:T(8,128)(2,1)S(1)}, u32[]{:S(2)}, u32[]{:S(2)}) collective-permute-start(bf16[1,128,256]{2,1,0:T(8,128)(2,1)} %rest_0_.5), channel_id=1, source_target_pairs={{0,8},{1,9},{2,10},{3,11},{4,12},{5,13},{6,14},{7,15},{8,0},{9,1},... | collective-permute-start | bytes 196616 | tf_op jit(solution)/shard_map/ppermute | solution.py:271
  3.8 1.2 %copy-done.1 = bf16[2,8,128,256]{3,2,1,0:T(8,128)(2,1)S(1)} copy-done((bf16[2,8,128,256]{3,2,1,0:T(8,128)(2,1)S(1)}, bf16[2,8,128,256]{3,2,1,0:T(8,128)(2,1)}, u32[]{:S(2)}) %copy-start.1) | copy-done | bytes 1048600
  5.1 0.8 %copy-done.2 = bf16[1,128,256]{2,1,0:T(8,128)(2,1)S(1)} copy-done((bf16[1,128,256]{2,1,0:T(8,128)(2,1)S(1)}, bf16[1,128,256]{2,1,0:T(8,128)(2,1)}, u32[]{:S(2)}) %copy-start.2) | copy-done | bytes 65560
  7.2 2.8 %pack.1 = (bf16[2,128,256]{2,1,0:T(8,128)(2,1)S(1)}, bf16[2,128,256]{2,1,0:T(8,128)(2,1)S(1)}, bf16[2,128,256]{2,1,0:T(8,128)(2,1)S(1)}, bf16[1,128,256]{2,1,0:T...) custom-call(s32[2,16]{1,0:T(2,128)S(1)} %copy-done.4, ...), custom_call_target="tpu_custom_call" | custom-call | tf_op jit(solution)/shard_map/pack/pallas_call | solution.py:65
  10.0 1.4 %collective-permute-start.5 = (bf16[2,128,256]{2,1,0:T(8,128)(2,1)S(1)}, bf16[2,128,256]{2,1,0:T(8,128)(2,1)S(1)}, u32[]{:S(2)}, u32[]{:S(2)}) collective-permute-start(bf16[2,128,256]{2,1,0:T(8,128)(2,1)S(1)} %get-tuple-element.26), channel_id=1, source_target_pairs={{0,4},{1,5},{2,6},{3,7},{4,0},{5,1},{6,2},{7,3},{8,12},{9,13},{10,... | collective-permute-start | bytes 393224 | tf_op jit(solution)/shard_map/ppermute | solution.py:271
  11.5 3.0 %collective-permute-start.14 = (bf16[1,128,256]{2,1,0:T(8,128)(2,1)S(1)}, bf16[1,128,256]{2,1,0:T(8,128)(2,1)S(1)}, u32[]{:S(2)}, u32[]{:S(2)}) collective-permute-start(bf16[1,128,256]{2,1,0:T(8,128)(2,1)S(1)} %get-tuple-element.33), channel_id=1, source_target_pairs={{0,5},{1,4},{2,7},{3,6},{4,1},{5,0},{6,3},{7,2},{8,13},{9,12},{10,... | collective-permute-start | bytes 196616 | tf_op jit(solution)/shard_map/ppermute | solution.py:271
  14.6 1.1 %collective-permute-start.15 = (bf16[1,128,256]{2,1,0:T(8,128)(2,1)S(1)}, bf16[1,128,256]{2,1,0:T(8,128)(2,1)S(1)}, u32[]{:S(2)}, u32[]{:S(2)}) collective-permute-start(bf16[1,128,256]{2,1,0:T(8,128)(2,1)S(1)} %get-tuple-element.34), channel_id=1, source_target_pairs={{0,6},{1,7},{2,4},{3,5},{4,2},{5,3},{6,0},{7,1},{8,14},{9,15},{10,... | collective-permute-start | bytes 196616 | tf_op jit(solution)/shard_map/ppermute | solution.py:271
  15.7 1.2 %collective-permute-done.6.rest_3_ = bf16[1,128,256]{2,1,0:T(8,128)(2,1)S(1)} collective-permute-done((bf16[1,128,256]{2,1,0:T(8,128)(2,1)S(1)}, bf16[1,128,256]{2,1,0:T(8,128)(2,1)S(1)}, u32[]{:S(2)}, u32[]{:S(2)}) %collective-permute-start.6) | collective-permute-done | bytes 65568 | tf_op jit(solution)/shard_map/ppermute | solution.py:271
  16.9 4.6 %collective-permute-start.16 = (bf16[1,128,256]{2,1,0:T(8,128)(2,1)S(1)}, bf16[1,128,256]{2,1,0:T(8,128)(2,1)S(1)}, u32[]{:S(2)}, u32[]{:S(2)}) collective-permute-start(bf16[1,128,256]{2,1,0:T(8,128)(2,1)S(1)} %get-tuple-element.35), channel_id=1, source_target_pairs={{0,7},{1,6},{2,5},{3,4},{4,3},{5,2},{6,1},{7,0},{8,15},{9,14},{10,... | collective-permute-start | bytes 196616 | tf_op jit(solution)/shard_map/ppermute | solution.py:271
  22.2 0.7 %collective-permute-start.7 = (bf16[3,128,256]{2,1,0:T(8,128)(2,1)S(1)}, bf16[3,128,256]{2,1,0:T(8,128)(2,1)S(1)}, u32[]{:S(2)}, u32[]{:S(2)}) collective-permute-start(bf16[3,128,256]{2,1,0:T(8,128)(2,1)S(1)} %get-tuple-element.27), channel_id=1, source_target_pairs={{0,1},{1,0},{2,3},{3,2},{4,5},{5,4},{6,7},{7,6},{8,9},{9,8},{10,11... | collective-permute-start | bytes 589832 | tf_op jit(solution)/shard_map/ppermute | solution.py:271
  23.6 3.6 %collective-permute-start.12 = (bf16[2,128,256]{2,1,0:T(8,128)(2,1)S(1)}, bf16[2,128,256]{2,1,0:T(8,128)(2,1)S(1)}, u32[]{:S(2)}, u32[]{:S(2)}) collective-permute-start(bf16[2,128,256]{2,1,0:T(8,128)(2,1)S(1)} %get-tuple-element.31), channel_id=1, source_target_pairs={{0,14},{1,15},{2,12},{3,13},{4,10},{5,11},{6,8},{7,9},{8,6},{9,7},... | collective-permute-start | bytes 393224 | tf_op jit(solution)/shard_map/ppermute | solution.py:271
  27.4 2.0 %collective-permute-start.9 = (bf16[3,128,256]{2,1,0:T(8,128)(2,1)S(1)}, bf16[3,128,256]{2,1,0:T(8,128)(2,1)S(1)}, u32[]{:S(2)}, u32[]{:S(2)}) collective-permute-start(bf16[3,128,256]{2,1,0:T(8,128)(2,1)S(1)} %get-tuple-element.29), channel_id=1, source_target_pairs={{0,3},{1,2},{2,1},{3,0},{4,7},{5,6},{6,5},{7,4},{8,11},{9,10},{10,... | collective-permute-start | bytes 589832 | tf_op jit(solution)/shard_map/ppermute | solution.py:271
  29.8 1.5 %collective-permute-start.11 = (bf16[2,128,256]{2,1,0:T(8,128)(2,1)S(1)}, bf16[2,128,256]{2,1,0:T(8,128)(2,1)S(1)}, u32[]{:S(2)}, u32[]{:S(2)}) collective-permute-start(bf16[2,128,256]{2,1,0:T(8,128)(2,1)S(1)} %collective-permute-done.10.rest_3_), channel_id=1, source_target_pairs={{0,1},{1,0},{2,3},{3,2},{4,5},{5,4},{6,7},{7,6},{8,9},{9,8},{10,11... | collective-permute-start | bytes 393224 | tf_op jit(solution)/shard_map/ppermute | solution.py:271
  31.3 2.2 %collective-permute-done.12.rest_5_ = bf16[2,128,256]{2,1,0:T(8,128)(2,1)S(1)} collective-permute-done((bf16[2,128,256]{2,1,0:T(8,128)(2,1)S(1)}, bf16[2,128,256]{2,1,0:T(8,128)(2,1)S(1)}, u32[]{:S(2)}, u32[]{:S(2)}) %collective-permute-start.12) | collective-permute-done | bytes 131104 | tf_op jit(solution)/shard_map/ppermute | solution.py:271
  33.6 1.1 %collective-permute-start.13 = (bf16[2,128,256]{2,1,0:T(8,128)(2,1)S(1)}, bf16[2,128,256]{2,1,0:T(8,128)(2,1)S(1)}, u32[]{:S(2)}, u32[]{:S(2)}) collective-permute-start(bf16[2,128,256]{2,1,0:T(8,128)(2,1)S(1)} %collective-permute-done.12.rest_5_), channel_id=1, source_target_pairs={{0,1},{1,0},{2,3},{3,2},{4,5},{5,4},{6,7},{7,6},{8,9},{9,8},{10,11... | collective-permute-start | bytes 393224 | tf_op jit(solution)/shard_map/ppermute | solution.py:271
  34.7 1.3 %collective-permute-done.8.rest_1_.rest_5_ = bf16[3,128,256]{2,1,0:T(8,128)(2,1)S(1)} collective-permute-done((bf16[3,128,256]{2,1,0:T(8,128)(2,1)S(1)}, bf16[3,128,256]{2,1,0:T(8,128)(2,1)S(1)}, u32[]{:S(2)}, u32[]{:S(2)}) %collective-permute-start.8) | collective-permute-done | bytes 196640 | tf_op jit(solution)/shard_map/ppermute | solution.py:271
  35.9 3.9 %collective-permute-start = (bf16[1,128,256]{2,1,0:T(8,128)(2,1)S(1)}, bf16[1,128,256]{2,1,0:T(8,128)(2,1)S(1)}, u32[]{:S(2)}, u32[]{:S(2)}) collective-permute-start(bf16[1,128,256]{2,1,0:T(8,128)(2,1)S(1)} %get-tuple-element.22), channel_id=1, source_target_pairs={{0,10},{1,11},{2,8},{3,9},{4,14},{5,15},{6,12},{7,13},{8,2},{9,3},... | collective-permute-start | bytes 196616 | tf_op jit(solution)/shard_map/ppermute | solution.py:271
  39.9 1.0 %collective-permute-done.9.rest_2_.rest_6_ = bf16[3,128,256]{2,1,0:T(8,128)(2,1)S(1)} collective-permute-done((bf16[3,128,256]{2,1,0:T(8,128)(2,1)S(1)}, bf16[3,128,256]{2,1,0:T(8,128)(2,1)S(1)}, u32[]{:S(2)}, u32[]{:S(2)}) %collective-permute-start.9) | collective-permute-done | bytes 196640 | tf_op jit(solution)/shard_map/ppermute | solution.py:271
  40.9 0.9 %collective-permute-start.1 = (bf16[1,128,256]{2,1,0:T(8,128)(2,1)S(1)}, bf16[1,128,256]{2,1,0:T(8,128)(2,1)S(1)}, u32[]{:S(2)}, u32[]{:S(2)}) collective-permute-start(bf16[1,128,256]{2,1,0:T(8,128)(2,1)S(1)} %get-tuple-element.23), channel_id=1, source_target_pairs={{0,11},{1,10},{2,9},{3,8},{4,15},{5,14},{6,13},{7,12},{8,3},{9,2},... | collective-permute-start | bytes 196616 | tf_op jit(solution)/shard_map/ppermute | solution.py:271
  41.8 2.5 %shard_map.77 = (f32[128,1024]{1,0:T(8,128)S(1)}, f32[8,1024]{1,0:T(8,128)S(1)}) custom-call(s32[2,16]{1,0:T(2,128)S(1)} %copy-done.4, s32[2]{0:T(128)S(1)} %copy-done.5, bf16[1,128,1024]{2,1,0:T(8,128)(2,1)S(1)} %copy-done, bf16[1,128,256]{2,1,0:T(8,128)(2,1)S(1)} %copy-done.3, bf16[1,128,256]{2,1,0:T(8,128)(2,1)S(1)} %get-tuple-element.32.rest_1_, ...), custom_call_target="tpu_custom_call" | custom-call | flops 402653184 | bytes 1048576 | tf_op jit(solution)/shard_map/pallas_call | solution.py:237
  44.3 1.4 %store.1 = bf16[1,8,128,256]{3,2,1,0:T(8,128)(2,1)} custom-call(s32[2,2]{1,0:T(2,128)S(1)} %copy-done.6, bf16[1,128,256]{2,1,0:T(8,128)(2,1)S(1)} %copy-done.3, bf16[1,128,256]{2,1,0:T(8,128)(2,1)S(1)} %collective-permute-done.4.rest_1_, bf16[2,128,256]{2,1,0:T(8,128)(2,1)S(1)} %collective-permute-done.5.rest_2_, ...), custom_call_target="tpu_custom_call" | custom-call | tf_op jit(solution)/shard_map/store/pallas_call | solution.py:149
  45.7 3.0 %shard_map.78 = (f32[128,1024]{1,0:T(8,128)S(1)}, f32[8,1024]{1,0:T(8,128)S(1)}) custom-call(s32[2,16]{1,0:T(2,128)S(1)} %copy-done.4, s32[2]{0:T(128)S(1)} %copy-done.5, bf16[1,128,1024]{2,1,0:T(8,128)(2,1)S(1)} %copy-done, bf16[3,128,256]{2,1,0:T(8,128)(2,1)S(1)} %collective-permute-done.7.rest_0_.rest_4_, ...), custom_call_target="tpu_custom_call" | custom-call | flops 536870912 | bytes 1048576 | tf_op jit(solution)/shard_map/pallas_call | solution.py:237
  48.7 1.2 %shard_map.79 = (f32[128,1024]{1,0:T(8,128)S(1)}, f32[8,1024]{1,0:T(8,128)S(1)}) custom-call(s32[2,16]{1,0:T(2,128)S(1)} %copy-done.4, s32[2]{0:T(128)S(1)} %copy-done.5, bf16[1,128,1024]{2,1,0:T(8,128)(2,1)S(1)} %copy-done, bf16[2,128,256]{2,1,0:T(8,128)(2,1)S(1)} %collective-permute-done.3.rest_0_, f32[128,1024]{1,0:T(8,128)S(1)} %get-tuple-element.38.rest_1_, ...), custom_call_target="tpu_custom_call" | custom-call | flops 67108864 | bytes 1048576 | tf_op jit(solution)/shard_map/pallas_call | solution.py:237
  49.9 2.5 %shard_map.80 = bf16[1,128,1024]{2,1,0:T(8,128)(2,1)} custom-call(s32[2,16]{1,0:T(2,128)S(1)} %copy-done.4, s32[2]{0:T(128)S(1)} %copy-done.5, bf16[1,128,1024]{2,1,0:T(8,128)(2,1)S(1)} %copy-done, bf16[1,128,256]{2,1,0:T(8,128)(2,1)S(1)} %collective-permute-done.rest_0_, bf16[1,128,256]{2,1,0:T(8,128)(2,1)S(1)} %collective-permute-done.1.rest_1_, ...), custom_call_target="tpu_custom_call" | custom-call | flops 134217728 | bytes 1048576 | tf_op jit(solution)/shard_map/pallas_call | solution.py:237
  (31 shorter events, 3.4 us)
Async XLA Ops:
  0.6 10.7 %collective-permute-start.4 = (bf16[1,128,256]{2,1,0:T(8,128)(2,1)}, bf16[1,128,256]{2,1,0:T(8,128)(2,1)S(1)}, u32[]{:S(2)}, u32[]{:S(2)}) collective-permute-start(bf16[1,128,256]{2,1,0:T(8,128)(2,1)} %rest_0_.5), channel_id=1, source_target_pairs={{0,8},{1,9},{2,10},{3,11},{4,12},{5,13},{6,14},{7,15},{8,0},{9,1},... | collective-permute-start | bytes 196616 | tf_op jit(solution)/shard_map/ppermute | solution.py:271
  3.8 1.2 %copy-start.1 = (bf16[2,8,128,256]{3,2,1,0:T(8,128)(2,1)S(1)}, bf16[2,8,128,256]{3,2,1,0:T(8,128)(2,1)}, u32[]{:S(2)}) copy-start(bf16[2,8,128,256]{3,2,1,0:T(8,128)(2,1)} %pool_ref.1) | copy-start | bytes 3145732
  5.0 0.8 %copy-start.2 = (bf16[1,128,256]{2,1,0:T(8,128)(2,1)S(1)}, bf16[1,128,256]{2,1,0:T(8,128)(2,1)}, u32[]{:S(2)}) copy-start(bf16[1,128,256]{2,1,0:T(8,128)(2,1)} %rest_0_.5) | copy-start | bytes 196612
  5.9 0.7 %copy-start.4 = (s32[2,16]{1,0:T(2,128)S(1)}, s32[2,16]{1,0:T(2,128)}, u32[]{:S(2)}) copy-start(s32[2,16]{1,0:T(2,128)} %hits_ref.9) | copy-start | bytes 388
  6.6 0.7 %copy-start.5 = (s32[2]{0:T(128)S(1)}, s32[2]{0:T(128)}, u32[]{:S(2)}) copy-start(s32[2]{0:T(128)} %blocks_ref.9) | copy-start | bytes 28
  7.2 14.3 %copy-start.3 = (bf16[1,128,256]{2,1,0:T(8,128)(2,1)S(1)}, bf16[1,128,256]{2,1,0:T(8,128)(2,1)}, u32[]{:S(2)}) copy-start(bf16[1,128,256]{2,1,0:T(8,128)(2,1)} %rest_0_.5) | copy-start | bytes 196612
  10.0 11.6 %collective-permute-start.5 = (bf16[2,128,256]{2,1,0:T(8,128)(2,1)S(1)}, bf16[2,128,256]{2,1,0:T(8,128)(2,1)S(1)}, u32[]{:S(2)}, u32[]{:S(2)}) collective-permute-start(bf16[2,128,256]{2,1,0:T(8,128)(2,1)S(1)} %get-tuple-element.26), channel_id=1, source_target_pairs={{0,4},{1,5},{2,6},{3,7},{4,0},{5,1},{6,2},{7,3},{8,12},{9,13},{10,... | collective-permute-start | bytes 393224 | tf_op jit(solution)/shard_map/ppermute | solution.py:271
  11.4 5.6 %collective-permute-start.6 = (bf16[1,128,256]{2,1,0:T(8,128)(2,1)S(1)}, bf16[1,128,256]{2,1,0:T(8,128)(2,1)S(1)}, u32[]{:S(2)}, u32[]{:S(2)}) collective-permute-start(bf16[1,128,256]{2,1,0:T(8,128)(2,1)S(1)} %collective-permute-done.4.rest_1_), channel_id=1, source_target_pairs={{0,4},{1,5},{2,6},{3,7},{4,0},{5,1},{6,2},{7,3},{8,12},{9,13},{10,... | collective-permute-start | bytes 196616 | tf_op jit(solution)/shard_map/ppermute | solution.py:271
  11.5 15.9 %collective-permute-start.2 = (bf16[2,128,256]{2,1,0:T(8,128)(2,1)S(1)}, bf16[2,128,256]{2,1,0:T(8,128)(2,1)S(1)}, u32[]{:S(2)}, u32[]{:S(2)}) collective-permute-start(bf16[2,128,256]{2,1,0:T(8,128)(2,1)S(1)} %get-tuple-element.24), channel_id=1, source_target_pairs={{0,8},{1,9},{2,10},{3,11},{4,12},{5,13},{6,14},{7,15},{8,0},{9,1},... | collective-permute-start | bytes 393224 | tf_op jit(solution)/shard_map/ppermute | solution.py:271
  11.5 11.4 %collective-permute-start.14 = (bf16[1,128,256]{2,1,0:T(8,128)(2,1)S(1)}, bf16[1,128,256]{2,1,0:T(8,128)(2,1)S(1)}, u32[]{:S(2)}, u32[]{:S(2)}) collective-permute-start(bf16[1,128,256]{2,1,0:T(8,128)(2,1)S(1)} %get-tuple-element.33), channel_id=1, source_target_pairs={{0,5},{1,4},{2,7},{3,6},{4,1},{5,0},{6,3},{7,2},{8,13},{9,12},{10,... | collective-permute-start | bytes 196616 | tf_op jit(solution)/shard_map/ppermute | solution.py:271
  14.6 9.0 %collective-permute-start.15 = (bf16[1,128,256]{2,1,0:T(8,128)(2,1)S(1)}, bf16[1,128,256]{2,1,0:T(8,128)(2,1)S(1)}, u32[]{:S(2)}, u32[]{:S(2)}) collective-permute-start(bf16[1,128,256]{2,1,0:T(8,128)(2,1)S(1)} %get-tuple-element.34), channel_id=1, source_target_pairs={{0,6},{1,7},{2,4},{3,5},{4,2},{5,3},{6,0},{7,1},{8,14},{9,15},{10,... | collective-permute-start | bytes 196616 | tf_op jit(solution)/shard_map/ppermute | solution.py:271
  16.9 4.7 %copy-start.6 = (s32[2,2]{1,0:T(2,128)S(1)}, s32[2,2]{1,0:T(2,128)}, u32[]{:S(2)}) copy-start(s32[2,2]{1,0:T(2,128)} %owners_ref.3) | copy-start | bytes 52
  16.9 10.3 %collective-permute-start.16 = (bf16[1,128,256]{2,1,0:T(8,128)(2,1)S(1)}, bf16[1,128,256]{2,1,0:T(8,128)(2,1)S(1)}, u32[]{:S(2)}, u32[]{:S(2)}) collective-permute-start(bf16[1,128,256]{2,1,0:T(8,128)(2,1)S(1)} %get-tuple-element.35), channel_id=1, source_target_pairs={{0,7},{1,6},{2,5},{3,4},{4,3},{5,2},{6,1},{7,0},{8,15},{9,14},{10,... | collective-permute-start | bytes 196616 | tf_op jit(solution)/shard_map/ppermute | solution.py:271
  21.6 20.2 %copy-start = (bf16[1,128,1024]{2,1,0:T(8,128)(2,1)S(1)}, bf16[1,128,1024]{2,1,0:T(8,128)(2,1)}, u32[]{:S(2)}) copy-start(bf16[1,128,1024]{2,1,0:T(8,128)(2,1)} %query_ref.7) | copy-start | bytes 786436
  22.2 12.4 %collective-permute-start.7 = (bf16[3,128,256]{2,1,0:T(8,128)(2,1)S(1)}, bf16[3,128,256]{2,1,0:T(8,128)(2,1)S(1)}, u32[]{:S(2)}, u32[]{:S(2)}) collective-permute-start(bf16[3,128,256]{2,1,0:T(8,128)(2,1)S(1)} %get-tuple-element.27), channel_id=1, source_target_pairs={{0,1},{1,0},{2,3},{3,2},{4,5},{5,4},{6,7},{7,6},{8,9},{9,8},{10,11... | collective-permute-start | bytes 589832 | tf_op jit(solution)/shard_map/ppermute | solution.py:271
  23.0 6.8 %collective-permute-start.10 = (bf16[2,128,256]{2,1,0:T(8,128)(2,1)S(1)}, bf16[2,128,256]{2,1,0:T(8,128)(2,1)S(1)}, u32[]{:S(2)}, u32[]{:S(2)}) collective-permute-start(bf16[2,128,256]{2,1,0:T(8,128)(2,1)S(1)} %get-tuple-element.30), channel_id=1, source_target_pairs={{0,12},{1,13},{2,14},{3,15},{4,8},{5,9},{6,10},{7,11},{8,4},{9,5},... | collective-permute-start | bytes 393224 | tf_op jit(solution)/shard_map/ppermute | solution.py:271
  23.6 10.0 %collective-permute-start.12 = (bf16[2,128,256]{2,1,0:T(8,128)(2,1)S(1)}, bf16[2,128,256]{2,1,0:T(8,128)(2,1)S(1)}, u32[]{:S(2)}, u32[]{:S(2)}) collective-permute-start(bf16[2,128,256]{2,1,0:T(8,128)(2,1)S(1)} %get-tuple-element.31), channel_id=1, source_target_pairs={{0,14},{1,15},{2,12},{3,13},{4,10},{5,11},{6,8},{7,9},{8,6},{9,7},... | collective-permute-start | bytes 393224 | tf_op jit(solution)/shard_map/ppermute | solution.py:271
  27.2 8.7 %collective-permute-start.8 = (bf16[3,128,256]{2,1,0:T(8,128)(2,1)S(1)}, bf16[3,128,256]{2,1,0:T(8,128)(2,1)S(1)}, u32[]{:S(2)}, u32[]{:S(2)}) collective-permute-start(bf16[3,128,256]{2,1,0:T(8,128)(2,1)S(1)} %get-tuple-element.28), channel_id=1, source_target_pairs={{0,2},{1,3},{2,0},{3,1},{4,6},{5,7},{6,4},{7,5},{8,10},{9,11},{10,... | collective-permute-start | bytes 589832 | tf_op jit(solution)/shard_map/ppermute | solution.py:271
  27.4 13.4 %collective-permute-start.9 = (bf16[3,128,256]{2,1,0:T(8,128)(2,1)S(1)}, bf16[3,128,256]{2,1,0:T(8,128)(2,1)S(1)}, u32[]{:S(2)}, u32[]{:S(2)}) collective-permute-start(bf16[3,128,256]{2,1,0:T(8,128)(2,1)S(1)} %get-tuple-element.29), channel_id=1, source_target_pairs={{0,3},{1,2},{2,1},{3,0},{4,7},{5,6},{6,5},{7,4},{8,11},{9,10},{10,... | collective-permute-start | bytes 589832 | tf_op jit(solution)/shard_map/ppermute | solution.py:271
  29.8 15.9 %collective-permute-start.11 = (bf16[2,128,256]{2,1,0:T(8,128)(2,1)S(1)}, bf16[2,128,256]{2,1,0:T(8,128)(2,1)S(1)}, u32[]{:S(2)}, u32[]{:S(2)}) collective-permute-start(bf16[2,128,256]{2,1,0:T(8,128)(2,1)S(1)} %collective-permute-done.10.rest_3_), channel_id=1, source_target_pairs={{0,1},{1,0},{2,3},{3,2},{4,5},{5,4},{6,7},{7,6},{8,9},{9,8},{10,11... | collective-permute-start | bytes 393224 | tf_op jit(solution)/shard_map/ppermute | solution.py:271
  33.6 12.1 %collective-permute-start.13 = (bf16[2,128,256]{2,1,0:T(8,128)(2,1)S(1)}, bf16[2,128,256]{2,1,0:T(8,128)(2,1)S(1)}, u32[]{:S(2)}, u32[]{:S(2)}) collective-permute-start(bf16[2,128,256]{2,1,0:T(8,128)(2,1)S(1)} %collective-permute-done.12.rest_5_), channel_id=1, source_target_pairs={{0,1},{1,0},{2,3},{3,2},{4,5},{5,4},{6,7},{7,6},{8,9},{9,8},{10,11... | collective-permute-start | bytes 393224 | tf_op jit(solution)/shard_map/ppermute | solution.py:271
  34.7 14.0 %collective-permute-start.3 = (bf16[2,128,256]{2,1,0:T(8,128)(2,1)S(1)}, bf16[2,128,256]{2,1,0:T(8,128)(2,1)S(1)}, u32[]{:S(2)}, u32[]{:S(2)}) collective-permute-start(bf16[2,128,256]{2,1,0:T(8,128)(2,1)S(1)} %collective-permute-done.2.rest_7_), channel_id=1, source_target_pairs={{0,1},{1,0},{2,3},{3,2},{4,5},{5,4},{6,7},{7,6},{8,9},{9,8},{10,11... | collective-permute-start | bytes 393224 | tf_op jit(solution)/shard_map/ppermute | solution.py:271
  35.9 14.0 %collective-permute-start = (bf16[1,128,256]{2,1,0:T(8,128)(2,1)S(1)}, bf16[1,128,256]{2,1,0:T(8,128)(2,1)S(1)}, u32[]{:S(2)}, u32[]{:S(2)}) collective-permute-start(bf16[1,128,256]{2,1,0:T(8,128)(2,1)S(1)} %get-tuple-element.22), channel_id=1, source_target_pairs={{0,10},{1,11},{2,8},{3,9},{4,14},{5,15},{6,12},{7,13},{8,2},{9,3},... | collective-permute-start | bytes 196616 | tf_op jit(solution)/shard_map/ppermute | solution.py:271
  40.9 9.1 %collective-permute-start.1 = (bf16[1,128,256]{2,1,0:T(8,128)(2,1)S(1)}, bf16[1,128,256]{2,1,0:T(8,128)(2,1)S(1)}, u32[]{:S(2)}, u32[]{:S(2)}) collective-permute-start(bf16[1,128,256]{2,1,0:T(8,128)(2,1)S(1)} %get-tuple-element.23), channel_id=1, source_target_pairs={{0,11},{1,10},{2,9},{3,8},{4,15},{5,14},{6,13},{7,12},{8,3},{9,2},... | collective-permute-start | bytes 196616 | tf_op jit(solution)/shard_map/ppermute | solution.py:271
